TPU v7x, 32 devices: a whole 2x2x4 slice. The times are simulated.
32 devices in a mesh: dp: 2 (over y), expert: 16 (over z, x, core).
Axes of the slice: x: 2, y: 2, z: 4, core: 2. Of those that a mesh axis runs over, the one named last changes fastest.
Arguments:
- tokens: bfloat16 [4096, 1024], P(('dp', 'expert')), may hold values from -6 to 6
- segments: int32 [4096], P(('dp', 'expert')), may hold values from 0 to 127, never falling along the last dimension, each value on 1 to 128 neighbouring positions
- routes: int32 [4096, 8], P(('dp', 'expert')), may hold values from 0 to 15, all different within a row; in each aligned block of 128 rows (0 to 127, 128 to 255, ...) at most 80 rows name the same one
- first_gain: bfloat16 [1024], P('dp'), may hold values from 0.5 to 1.5
- query_weight: bfloat16 [1024, 1024], P('dp'), may hold values from -0.75 to 0.75
- key_projection_weight: bfloat16 [1024, 512], P('dp'), may hold values from -0.75 to 0.75
- value_projection_weight: bfloat16 [1024, 512], P('dp'), may hold values from -0.1875 to 0.1875
- out_weight: bfloat16 [1024, 1024], P('dp'), may hold values from -0.75 to 0.75
- second_gain: bfloat16 [1024], P('dp'), may hold values from 0.5 to 1.5
- router_weight: bfloat16 [1024, 16], P('dp'), may hold values from -0.375 to 0.375
- gate_weight: bfloat16 [16, 1024, 512], P('expert'), may hold values from -0.1875 to 0.1875
- up_weight: bfloat16 [16, 1024, 512], P('expert'), may hold values from -0.1875 to 0.1875
- down_weight: bfloat16 [16, 512, 1024], P('expert'), may hold values from -0.5 to 0.5
- cotangent: bfloat16 [4096, 1024], P(('dp', 'expert')), may hold values from -6 to 6
Outputs:
- output: bfloat16 [4096, 1024], P(('dp', 'expert'))
- grad_tokens: float32 [4096, 1024], P(('dp', 'expert'))
- first_gain_grad: float32 [1024], P('dp')
- query_weight_grad: float32 [1024, 1024], P('dp')
- key_weight_grad: float32 [1024, 512], P('dp')
- value_weight_grad: float32 [1024, 512], P('dp')
- out_weight_grad: float32 [1024, 1024], P('dp')
- second_gain_grad: float32 [1024], P('dp')
- router_weight_grad: float32 [1024, 16], P('dp')
- gate_weight_grad: float32 [16, 1024, 512], P('expert', 'dp')
- up_weight_grad: float32 [16, 1024, 512], P('expert', 'dp')
- down_weight_grad: float32 [16, 512, 1024], P('expert', None, 'dp')
Inputs may be any that keep to these rules, and one draw needn't show every extreme that they name: `routes`: within the rows of one device (aligned blocks of 128 tokens) no expert is named by more than 80 rows; in some block one expert is named by exactly 80. A row names 8 different experts. `segments`: segment numbers never fall along the tokens; a segment holds 1 to 128 tokens and one holds exactly 128.
All inputs are finite; a program needn't handle non-finite values.
Results may differ from a plain program's by a relative error of at most 0.02.
The roundings to bfloat16 on the way count: a program that leaves them out, or rounds other values in their place, can miss the bound.
Values may be sent and summed in bfloat16 or wider, within the bound.
A program may use at most 128 MiB of HBM per device.

v0:
```python
import jax
import jax.numpy as jnp
from jax import lax
from jax.sharding import PartitionSpec as P

QUERY_HEADS = 16
KEY_VALUE_HEADS = 8
HEAD_DIM = 64
SEQUENCE_LENGTH = 128


EPSILON = 1e-06
SCORE_SCALE = 0.015625
ROPE_BASE = 10000.0
MASKED = -1e30


def product(pattern, left_op, right_op):
    return jnp.einsum(pattern, left_op, right_op, preferred_element_type=jnp.float32)


def matrix_multiply(left_op, right_op):
    return jnp.dot(left_op, right_op, preferred_element_type=jnp.float32)


def rope_tables(seq_len, head_size):
    positions = jnp.arange(seq_len, dtype=jnp.float32)
    exponent = jnp.arange(head_size // 2, dtype=jnp.float32) * (2.0 / head_size)
    angles = positions[:, None] * (ROPE_BASE ** (-exponent))[None, :]
    return (jnp.cos(angles)[None, :, None, :], jnp.sin(angles)[None, :, None, :])


def apply_rotary(values, cosine_table, sine_table):
    middle = values.shape[-1] // 2
    first_half = values[..., :middle]
    second_half = values[..., middle:]
    return jnp.concatenate(
        [
            first_half * cosine_table - second_half * sine_table,
            second_half * cosine_table + first_half * sine_table,
        ],
        -1,
    )


def inverse_rotary(gradient, cosine_table, sine_table):
    middle = gradient.shape[-1] // 2
    first_half = gradient[..., :middle]
    second_half = gradient[..., middle:]
    return jnp.concatenate(
        [
            first_half * cosine_table + second_half * sine_table,
            second_half * cosine_table - first_half * sine_table,
        ],
        -1,
    )


def normalize(values, gain_vec):
    factor = lax.rsqrt(jnp.mean(values * values, -1, keepdims=True) + EPSILON)
    normed = values * factor
    return (normed, factor, (normed * gain_vec).astype(jnp.bfloat16))


def normalize_back(gradient, normed, factor, gain_vec):
    gain_grad = jnp.sum(gradient * normed, 0)
    scaled = gradient * gain_vec
    return (factor * (scaled - normed * jnp.mean(scaled * normed, -1, keepdims=True)), gain_grad)


def segment_mask(segments):
    seq_len = segments.shape[1]
    causal = jnp.arange(seq_len)[:, None] >= jnp.arange(seq_len)[None, :]
    same_doc = segments[:, :, None] == segments[:, None, :]
    return (same_doc & causal[None])[:, None, None]


def score_table(query_rows, key_row_block, mask_tab):
    raw_scores = product("sqhgw,skhw->shgqk", query_rows, key_row_block) * SCORE_SCALE
    return jnp.where(mask_tab, raw_scores, MASKED)


def mixer_forward(tokens, segments, gain_vec, query_mat, key_matrix, value_matrix, out_mat):
    token_rows = tokens.shape[0]
    local_sequences = token_rows // SEQUENCE_LENGTH
    query_groups = QUERY_HEADS // KEY_VALUE_HEADS
    cosine_table, sine_table = rope_tables(SEQUENCE_LENGTH, HEAD_DIM)
    mask_tab = segment_mask(segments.reshape(local_sequences, SEQUENCE_LENGTH))
    residual = tokens.astype(jnp.float32)
    normed, factor, attention_input = normalize(residual, gain_vec)
    query_rows = apply_rotary(
        matrix_multiply(attention_input, query_mat).reshape(
            local_sequences, SEQUENCE_LENGTH, QUERY_HEADS, HEAD_DIM
        ),
        cosine_table,
        sine_table,
    )
    query_rows = query_rows.astype(jnp.bfloat16).reshape(
        local_sequences, SEQUENCE_LENGTH, KEY_VALUE_HEADS, query_groups, HEAD_DIM
    )
    key_row_block = apply_rotary(
        matrix_multiply(attention_input, key_matrix).reshape(
            local_sequences, SEQUENCE_LENGTH, KEY_VALUE_HEADS, HEAD_DIM
        ),
        cosine_table,
        sine_table,
    ).astype(jnp.bfloat16)
    value_row_block = (
        matrix_multiply(attention_input, value_matrix)
        .astype(jnp.bfloat16)
        .reshape(local_sequences, SEQUENCE_LENGTH, KEY_VALUE_HEADS, HEAD_DIM)
    )
    scores = score_table(query_rows, key_row_block, mask_tab)
    row_peak = jnp.max(scores, -1, keepdims=True)
    logsum = row_peak + jnp.log(jnp.sum(jnp.exp(scores - row_peak), -1, keepdims=True))
    weights = jnp.exp(scores - logsum).astype(jnp.bfloat16)
    attended = product("shgqk,skhw->sqhgw", weights, value_row_block).astype(jnp.bfloat16)
    hidden = residual + matrix_multiply(
        attended.reshape(token_rows, QUERY_HEADS * HEAD_DIM), out_mat
    )
    saved = (
        normed,
        factor,
        attention_input,
        query_rows,
        key_row_block,
        value_row_block,
        attended,
        logsum,
        mask_tab,
        cosine_table,
        sine_table,
    )
    return (hidden, saved)


def mixer_backward(grad_hidden, saved, gain_vec, query_mat, key_matrix, value_matrix, out_mat):
    (
        normed,
        factor,
        attention_input,
        query_rows,
        key_row_block,
        value_row_block,
        attended,
        logsum,
        mask_tab,
        cosine_table,
        sine_table,
    ) = saved
    token_rows = grad_hidden.shape[0]
    local_sequences = token_rows // SEQUENCE_LENGTH
    grad_round = grad_hidden.astype(jnp.bfloat16)
    out_grad = matrix_multiply(attended.reshape(token_rows, QUERY_HEADS * HEAD_DIM).T, grad_round)
    grad_attended = (
        matrix_multiply(grad_round, out_mat.T).astype(jnp.bfloat16).reshape(query_rows.shape)
    )
    scores = score_table(query_rows, key_row_block, mask_tab)
    prob_full = jnp.exp(scores - logsum)
    values_gradient = product("shgqk,sqhgw->skhw", prob_full.astype(jnp.bfloat16), grad_attended)
    grad_weights = product("sqhgw,skhw->shgqk", grad_attended, value_row_block)
    row_delta = product("sqhgw,sqhgw->shgq", grad_attended, attended)[..., None]
    grad_scores = (prob_full * (grad_weights - row_delta) * SCORE_SCALE).astype(jnp.bfloat16)
    grad_queries = product("shgqk,skhw->sqhgw", grad_scores, key_row_block)
    keys_gradient = product("shgqk,sqhgw->skhw", grad_scores, query_rows)
    query_grad = inverse_rotary(
        grad_queries.reshape(local_sequences, SEQUENCE_LENGTH, QUERY_HEADS, HEAD_DIM),
        cosine_table,
        sine_table,
    )
    query_grad = query_grad.astype(jnp.bfloat16).reshape(token_rows, QUERY_HEADS * HEAD_DIM)
    key_gradient = (
        inverse_rotary(keys_gradient, cosine_table, sine_table)
        .astype(jnp.bfloat16)
        .reshape(token_rows, KEY_VALUE_HEADS * HEAD_DIM)
    )
    value_gradient = values_gradient.astype(jnp.bfloat16).reshape(
        token_rows, KEY_VALUE_HEADS * HEAD_DIM
    )
    query_wgrad = matrix_multiply(attention_input.T, query_grad)
    key_wgrad = matrix_multiply(attention_input.T, key_gradient)
    value_wgrad = matrix_multiply(attention_input.T, value_gradient)
    grad_attn_input = (
        matrix_multiply(query_grad, query_mat.T)
        + matrix_multiply(key_gradient, key_matrix.T)
        + matrix_multiply(value_gradient, value_matrix.T)
    )
    grad_normed, gain_grad = normalize_back(grad_attn_input, normed, factor, gain_vec)
    return (grad_hidden + grad_normed, gain_grad, query_wgrad, key_wgrad, value_wgrad, out_grad)


def route_weights(expert_input, router_mat, routes):
    logits = matrix_multiply(expert_input, router_mat)
    chosen_hot = (
        routes[:, :, None] == jnp.arange(router_mat.shape[1], dtype=jnp.int32)[None, None, :]
    ).astype(jnp.float32)
    chosen = jnp.sum(chosen_hot * logits[:, None, :], -1)
    return (jax.nn.softmax(chosen, -1), chosen_hot)


def route_back(route_prob, grad_prob, chosen_hot):
    grad_chosen = route_prob * (grad_prob - jnp.sum(route_prob * grad_prob, -1, keepdims=True))
    return jnp.sum(chosen_hot * grad_chosen[:, :, None], 1).astype(jnp.bfloat16)


def expert_forward(owner_rows, gate_mat, up_mat, down_mat):
    gate_pre = product("erd,edf->erf", owner_rows, gate_mat)
    up_pre = product("erd,edf->erf", owner_rows, up_mat)
    gate_sig = jax.nn.sigmoid(gate_pre)
    gate_act = gate_pre * gate_sig
    inner_acts = (gate_act * up_pre).astype(jnp.bfloat16)
    expert_out = product("erf,efd->erd", inner_acts, down_mat).astype(jnp.bfloat16)
    return (expert_out, (gate_pre, up_pre, gate_sig, gate_act, inner_acts))


def expert_backward(grad_rows, owner_rows, kept_acts, gate_mat, up_mat, down_mat):
    gate_pre, up_pre, gate_sig, gate_act, inner_acts = kept_acts
    grad_inner = product("erd,efd->erf", grad_rows, down_mat)
    down_grad = product("erf,erd->efd", inner_acts, grad_rows)
    silu_slope = gate_sig * (1.0 + gate_pre * (1.0 - gate_sig))
    grad_gate = (grad_inner * up_pre * silu_slope).astype(jnp.bfloat16)
    grad_up = (grad_inner * gate_act).astype(jnp.bfloat16)
    gate_grad = product("erd,erf->edf", owner_rows, grad_gate)
    up_grad = product("erd,erf->edf", owner_rows, grad_up)
    grad_owner_rows = product("erf,edf->erd", grad_gate, gate_mat) + product(
        "erf,edf->erd", grad_up, up_mat
    )
    return (grad_owner_rows.astype(jnp.bfloat16), gate_grad, up_grad, down_grad)


def to_owner(arrived, owner_count, local_count):
    capacity = arrived.shape[1]
    model_width = arrived.shape[2]
    shaped = arrived.reshape(owner_count, local_count, capacity, model_width).transpose(1, 0, 2, 3)
    return shaped.reshape(local_count, owner_count * capacity, model_width)


def to_source(owner_rows, owner_count, local_count, capacity):
    model_width = owner_rows.shape[2]
    shaped = owner_rows.reshape(local_count, owner_count, capacity, model_width).transpose(
        1, 0, 2, 3
    )
    return shaped.reshape(owner_count * local_count, capacity, model_width)


def shards(
    tokens,
    segments,
    routes,
    first_gain,
    query_weight,
    key_projection_weight,
    value_projection_weight,
    out_weight,
    second_gain,
    router_weight,
    gate_weight,
    up_weight,
    down_weight,
    cotangent,
):
    gathered = (
        lax.all_gather(query_weight, "dp", axis=0, tiled=True),
        lax.all_gather(key_projection_weight, "dp", axis=0, tiled=True),
        lax.all_gather(value_projection_weight, "dp", axis=0, tiled=True),
        lax.all_gather(out_weight, "dp", axis=0, tiled=True),
        lax.all_gather(router_weight, "dp", axis=0, tiled=True),
        lax.all_gather(first_gain, "dp", axis=0, tiled=True),
        lax.all_gather(second_gain, "dp", axis=0, tiled=True),
    )
    query_mat, key_matrix, value_matrix, out_mat, router_mat, gain_first, gain_second = gathered
    token_rows = tokens.shape[0]
    model_width = tokens.shape[1]
    top_count = routes.shape[1]
    expert_count = router_mat.shape[1]
    owner_count = lax.axis_size("expert")
    local_count = gate_weight.shape[0]
    capacity = 5 * token_rows * top_count // (4 * expert_count)
    hidden, saved = mixer_forward(
        tokens, segments, gain_first, query_mat, key_matrix, value_matrix, out_mat
    )
    normed_second, factor_second, expert_input = normalize(hidden, gain_second)
    route_prob, chosen_hot = route_weights(expert_input, router_mat, routes)
    flat_routes = routes.reshape(-1)
    route_hot = (flat_routes[:, None] == jnp.arange(expert_count, dtype=jnp.int32)[None, :]).astype(
        jnp.int32
    )
    slot_of = jnp.sum(route_hot * jnp.cumsum(route_hot, 0), 1) - 1
    target = flat_routes * capacity + slot_of
    entries = (
        jnp.full((expert_count * capacity,), -1, jnp.int32)
        .at[target]
        .set(jnp.arange(token_rows * top_count, dtype=jnp.int32))
    )
    live_slot = entries >= 0
    source = jnp.maximum(entries, 0)
    send_rows = jnp.where(
        live_slot[:, None], expert_input[source // top_count], jnp.zeros((), jnp.bfloat16)
    )
    arrived = lax.all_to_all(
        send_rows.reshape(expert_count, capacity, model_width),
        "expert",
        split_axis=0,
        concat_axis=0,
        tiled=True,
    )
    owner_rows = to_owner(arrived, owner_count, local_count)
    expert_out, kept_acts = expert_forward(owner_rows, gate_weight, up_weight, down_weight)
    returned = lax.all_to_all(
        to_source(expert_out, owner_count, local_count, capacity),
        "expert",
        split_axis=0,
        concat_axis=0,
        tiled=True,
    )
    out_rows = returned.reshape(expert_count * capacity, model_width)[target]
    out_rows = out_rows.reshape(token_rows, top_count, model_width).astype(jnp.float32)
    output = (hidden + jnp.sum(route_prob[:, :, None] * out_rows, 1)).astype(jnp.bfloat16)
    grad_output = cotangent.astype(jnp.float32)
    grad_pairs = (
        (route_prob[:, :, None] * grad_output[:, None, :])
        .astype(jnp.bfloat16)
        .reshape(token_rows * top_count, model_width)
    )
    grad_prob = jnp.sum(out_rows * grad_output[:, None, :], -1)
    grad_send = jnp.where(live_slot[:, None], grad_pairs[source], jnp.zeros((), jnp.bfloat16))
    grad_arrived = lax.all_to_all(
        grad_send.reshape(expert_count, capacity, model_width),
        "expert",
        split_axis=0,
        concat_axis=0,
        tiled=True,
    )
    grad_owner_rows, gate_grad, up_grad, down_grad = expert_backward(
        to_owner(grad_arrived, owner_count, local_count),
        owner_rows,
        kept_acts,
        gate_weight,
        up_weight,
        down_weight,
    )
    grad_back = lax.all_to_all(
        to_source(grad_owner_rows, owner_count, local_count, capacity),
        "expert",
        split_axis=0,
        concat_axis=0,
        tiled=True,
    )
    grad_pair_rows = grad_back.reshape(expert_count * capacity, model_width)[target]
    grad_expert_input = jnp.sum(
        grad_pair_rows.reshape(token_rows, top_count, model_width).astype(jnp.float32), 1
    )
    expert_shares = (
        lax.psum_scatter(
            gate_grad.astype(jnp.bfloat16), "dp", scatter_dimension=1, tiled=True
        ).astype(jnp.float32),
        lax.psum_scatter(
            up_grad.astype(jnp.bfloat16), "dp", scatter_dimension=1, tiled=True
        ).astype(jnp.float32),
        lax.psum_scatter(
            down_grad.astype(jnp.bfloat16), "dp", scatter_dimension=2, tiled=True
        ).astype(jnp.float32),
    )
    router_grad = route_back(route_prob, grad_prob, chosen_hot)
    grad_expert_input = grad_expert_input + matrix_multiply(router_grad, router_mat.T)
    router_wgrad = matrix_multiply(expert_input.T, router_grad)
    grad_normed, second_gain_grad = normalize_back(
        grad_expert_input, normed_second, factor_second, gain_second
    )
    grad_hidden = grad_output + grad_normed
    grad_tokens, first_gain_grad, query_wgrad, key_wgrad, value_wgrad, out_wgrad = mixer_backward(
        grad_hidden, saved, gain_first, query_mat, key_matrix, value_matrix, out_mat
    )
    partials = (
        query_wgrad,
        key_wgrad,
        value_wgrad,
        out_wgrad,
        router_wgrad,
        first_gain_grad,
        second_gain_grad,
    )
    pieces = (
        lax.psum_scatter(
            partials[0].astype(jnp.bfloat16), "dp", scatter_dimension=0, tiled=True
        ).astype(jnp.float32),
        lax.psum_scatter(
            partials[1].astype(jnp.bfloat16), "dp", scatter_dimension=0, tiled=True
        ).astype(jnp.float32),
        lax.psum_scatter(
            partials[2].astype(jnp.bfloat16), "dp", scatter_dimension=0, tiled=True
        ).astype(jnp.float32),
        lax.psum_scatter(
            partials[3].astype(jnp.bfloat16), "dp", scatter_dimension=0, tiled=True
        ).astype(jnp.float32),
        lax.psum_scatter(
            partials[4].astype(jnp.bfloat16), "dp", scatter_dimension=0, tiled=True
        ).astype(jnp.float32),
        lax.psum_scatter(
            partials[5].astype(jnp.bfloat16), "dp", scatter_dimension=0, tiled=True
        ).astype(jnp.float32),
        lax.psum_scatter(
            partials[6].astype(jnp.bfloat16), "dp", scatter_dimension=0, tiled=True
        ).astype(jnp.float32),
    )
    shares = (
        lax.psum(pieces[0].astype(jnp.bfloat16), "expert").astype(jnp.float32),
        lax.psum(pieces[1].astype(jnp.bfloat16), "expert").astype(jnp.float32),
        lax.psum(pieces[2].astype(jnp.bfloat16), "expert").astype(jnp.float32),
        lax.psum(pieces[3].astype(jnp.bfloat16), "expert").astype(jnp.float32),
        lax.psum(pieces[4].astype(jnp.bfloat16), "expert").astype(jnp.float32),
        lax.psum(pieces[5].astype(jnp.bfloat16), "expert").astype(jnp.float32),
        lax.psum(pieces[6].astype(jnp.bfloat16), "expert").astype(jnp.float32),
    )
    query_share, key_share, value_share, out_share, router_share, first_share, second_share = shares
    return (
        output,
        grad_tokens,
        first_share,
        query_share,
        key_share,
        value_share,
        out_share,
        second_share,
        router_share,
        expert_shares[0],
        expert_shares[1],
        expert_shares[2],
    )


def solution(mesh):
    placed = (
        P(("dp", "expert"), None),
        P(("dp", "expert")),
        P(("dp", "expert"), None),
        P("dp"),
        P("dp", None),
        P("dp", None),
        P("dp", None),
        P("dp", None),
        P("dp"),
        P("dp", None),
        P("expert", None, None),
        P("expert", None, None),
        P("expert", None, None),
        P(("dp", "expert"), None),
    )
    return jax.shard_map(
        shards,
        mesh=mesh,
        in_specs=placed,
        out_specs=(
            P(("dp", "expert"), None),
            P(("dp", "expert"), None),
            P("dp"),
            P("dp", None),
            P("dp", None),
            P("dp", None),
            P("dp", None),
            P("dp"),
            P("dp", None),
            P("expert", "dp", None),
            P("expert", "dp", None),
            P("expert", None, "dp"),
        ),
        check_vma=False,
    )
```

profile of v0, /device:TPU:0, one launch (start us, length us, event | category | flops | bytes accessed | tf_op | source)
XLA Modules:
  0.0 741.7 jit_solution(16114862467862968674)
XLA Ops:
  10.6 4.5 reduce-window.6
  15.6 4.3 scatter_custom_fusion
  20.2 5.5 all-gather
  25.7 4.5 all-gather.1
  30.5 4.4 all_gather.27
  38.7 18.1 %all-gather.9.cloned.1.call-done = bf16[1024,512]{1,0:T(8,128)(2,1)} async-done(((bf16[512,512]{1,0:T(8,128)(2,1)}), bf16[1024,512]{1,0:T(8,128)(2,1)}) %all-gather.9.cloned.1.call-update) | async-done | bytes 1048592 | tf_op jit(solution)/shard_map/all_gather | solution.py:264
  58.7 32.8 %all-gather.11.cloned.1.call-done = bf16[1024,1024]{1,0:T(8,128)(2,1)} async-done(((bf16[512,1024]{1,0:T(8,128)(2,1)}), bf16[1024,1024]{1,0:T(8,128)(2,1)}) %all-gather.11.cloned.1.call-update) | async-done | bytes 2097168 | tf_op jit(solution)/shard_map/all_gather | solution.py:263
  96.5 29.5 %all-gather.13.cloned.1.call-done = bf16[1024,1024]{1,0:T(8,128)(2,1)} async-done(((bf16[512,1024]{1,0:T(8,128)(2,1)}), bf16[1024,1024]{1,0:T(8,128)(2,1)}) %all-gather.13.cloned.1.call-update) | async-done | bytes 2097168 | tf_op jit(solution)/shard_map/all_gather | solution.py:266
  131.3 5.1 gather_fusion
  137.7 5.3 gather_fusion.2
  146.8 63.9 %all_to_all.20 = bf16[16,80,1024]{2,1,0:T(8,128)(2,1)} all-to-all(bf16[16,80,1024]{2,1,0:T(8,128)(2,1)S(1)} %get-tuple-element.43), channel_id=1, replica_groups=mesh['dp'=2,'expert'=16] {'expert'}, dimensions={0} | all-to-all | bytes 5242880 | tf_op jit(solution)/shard_map/all_to_all | solution.py:300
  210.7 5.4 all-to-all-start.2
  216.1 5.0 fusion.19
  224.2 42.0 %all-to-all-done.2 = bf16[16,80,1024]{2,1,0:T(8,128)(2,1)} async-done(((bf16[16,80,1024]{2,1,0:T(8,128)(2,1)}), bf16[16,80,1024]{2,1,0:T(8,128)(2,1)}, u32[]{:S(2)}, u32[]{:S(2)}) %all-to-all-start.2) | async-done | bytes 2621472 | tf_op jit(solution)/shard_map/all_to_all | solution.py:327
  266.2 7.0 multiply_convert_fusion
  276.3 13.4 %all-to-all-start.1 = ((bf16[16,80,1024]{2,1,0:T(8,128)(2,1)}), bf16[16,80,1024]{2,1,0:T(8,128)(2,1)}, u32[]{:S(2)}, u32[]{:S(2)}) async-start(bf16[16,80,1024]{2,1,0:T(8,128)(2,1)} %bitcast.202), calls=%async_computation.1 | async-start | bytes 5242880 | tf_op jit(solution)/shard_map/all_to_all | solution.py:309
  296.1 43.8 %all-to-all-done.1 = bf16[16,80,1024]{2,1,0:T(8,128)(2,1)} async-done(((bf16[16,80,1024]{2,1,0:T(8,128)(2,1)}), bf16[16,80,1024]{2,1,0:T(8,128)(2,1)}, u32[]{:S(2)}, u32[]{:S(2)}) %all-to-all-start.1) | async-done | bytes 2621472 | tf_op jit(solution)/shard_map/all_to_all | solution.py:309
  339.9 13.5 %all-to-all-start.3 = ((bf16[16,80,1024]{2,1,0:T(8,128)(2,1)}), bf16[16,80,1024]{2,1,0:T(8,128)(2,1)}, u32[]{:S(2)}, u32[]{:S(2)}) async-start(bf16[16,80,1024]{2,1,0:T(8,128)(2,1)} %bitcast.191), calls=%async_computation.3 | async-start | bytes 5242880 | tf_op jit(solution)/shard_map/all_to_all | solution.py:342
  353.7 7.1 gather_fusion.1
  363.4 40.2 %all-to-all-done.3 = bf16[16,80,1024]{2,1,0:T(8,128)(2,1)} async-done(((bf16[16,80,1024]{2,1,0:T(8,128)(2,1)}), bf16[16,80,1024]{2,1,0:T(8,128)(2,1)}, u32[]{:S(2)}, u32[]{:S(2)}) %all-to-all-start.3) | async-done | bytes 2621472 | tf_op jit(solution)/shard_map/all_to_all | solution.py:342
  403.5 7.1 gather_fusion.3
  427.4 4.7 fusion.6
  436.9 4.6 fusion.4
  445.3 23.1 %reduce-scatter.11.cloned.1.call-done = bf16[512,512]{1,0:T(8,128)(2,1)} async-done(((bf16[1024,512]{1,0:T(8,128)(2,1)}), bf16[512,512]{1,0:T(8,128)(2,1)}) %reduce-scatter.11.cloned.1.call-update) | async-done | bytes 524304 | tf_op jit(solution)/shard_map/reduce_scatter | solution.py:387
  468.4 34.7 %reduce-scatter.15.cloned.1.call-done = bf16[512,1024]{1,0:T(8,128)(2,1)} async-done(((bf16[1024,1024]{1,0:T(8,128)(2,1)}), bf16[512,1024]{1,0:T(8,128)(2,1)}) %reduce-scatter.15.cloned.1.call-update) | async-done | bytes 1048592 | tf_op jit(solution)/shard_map/reduce_scatter | solution.py:393
  503.1 34.8 %reduce-scatter.9.cloned.1.call-done = bf16[512,1024]{1,0:T(8,128)(2,1)} async-done(((bf16[1024,1024]{1,0:T(8,128)(2,1)}), bf16[512,1024]{1,0:T(8,128)(2,1)}) %reduce-scatter.9.cloned.1.call-update) | async-done | bytes 1048592 | tf_op jit(solution)/shard_map/reduce_scatter | solution.py:384
  539.2 21.9 %reduce-scatter.23.cloned.1.call-done = bf16[1,512,512]{2,1,0:T(8,128)(2,1)} async-done(((bf16[1,512,1024]{2,1,0:T(8,128)(2,1)}), bf16[1,512,512]{2,1,0:T(8,128)(2,1)}) %reduce-scatter.23.cloned.1.call-update) | async-done | bytes 524304 | tf_op jit(solution)/shard_map/reduce_scatter | solution.py:360
  563.3 20.9 %reduce-scatter.21.cloned.1.call-done = bf16[1,512,512]{2,1,0:T(8,128)(2,1)} async-done(((bf16[1,1024,512]{2,1,0:T(8,128)(2,1)}), bf16[1,512,512]{2,1,0:T(8,128)(2,1)}) %reduce-scatter.21.cloned.1.call-update) | async-done | bytes 524304 | tf_op jit(solution)/shard_map/reduce_scatter | solution.py:357
  586.3 21.1 %reduce-scatter.19.cloned.1.call-done = bf16[1,512,512]{2,1,0:T(8,128)(2,1)} async-done(((bf16[1,1024,512]{2,1,0:T(8,128)(2,1)}), bf16[1,512,512]{2,1,0:T(8,128)(2,1)}) %reduce-scatter.19.cloned.1.call-update) | async-done | bytes 524304 | tf_op jit(solution)/shard_map/reduce_scatter | solution.py:354
  611.6 4.9 all-reduce.4
  620.0 61.4 %all-reduce.2 = (bf16[512]{0:T(512)(128)(2,1)S(1)}, bf16[512]{0:T(512)(128)(2,1)S(1)}, bf16[512,16]{0,1:T(8,128)(2,1)S(1)}) all-reduce(bf16[512]{0:T(512)(128)(2,1)S(1)} %dynamic-slice.1, bf16[512]{0:T(512)(128)(2,1)S(1)} %dynamic-slice.3, ...), channel_id=1, replica_groups=mesh['dp'=2,'expert'=16] {'expert'}, use_global_device_ids=true, to_apply=%region_20.21 | all-reduce | flops 9216 | bytes 36864 | tf_op jit(solution)/shard_map/psum | solution.py:412
  683.2 45.3 %all-reduce.7.cloned.1.call-done = (bf16[512,1024]{1,0:T(8,128)(2,1)}, bf16[512,512]{1,0:T(8,128)(2,1)}, bf16[512,512]{1,0:T(8,128)(2,1)}, bf16[512,1024]{1,0:T(8,128)(2,1)}) async-done(((bf16[512,1024]{1,0:T(8,128)(2,1)}, bf16[512,512]{1,0:T(8,128)(2,1)}, bf16[512,512]{1,0:T(8,128)(2,1)}, bf16[512,1024]{1,0:T(8,128)(2,1)}), (bf16[512,1024]{1,0:T(8,128)(2,1)}, bf16[512,512]{1,0:T(8,128)(2,1)}, ...) | async-done | bytes 3145744 | tf_op jit(solution)/shard_map/psum | solution.py:407
  (273 shorter events, 86.3 us)
Async XLA Ops:
  7.2 259.1 %copy-start = (bf16[1,512,1024]{2,1,0:T(8,128)(2,1)S(1)}, bf16[1,512,1024]{2,1,0:T(8,128)(2,1)}, u32[]{:S(2)}) copy-start(bf16[1,512,1024]{2,1,0:T(8,128)(2,1)} %param.26) | copy-start | bytes 3145732
  7.2 23.2 %copy-start.56 = (bf16[512,16]{0,1:T(8,128)(2,1)S(1)}, bf16[512,16]{0,1:T(8,128)(2,1)}, u32[]{:S(2)}) copy-start(bf16[512,16]{0,1:T(8,128)(2,1)} %param.23) | copy-start | bytes 49156
  7.3 28.3 %copy-start.23 = (bf16[128,1024]{1,0:T(8,128)(2,1)S(1)}, bf16[128,1024]{1,0:T(8,128)(2,1)}, u32[]{:S(2)}) copy-start(bf16[128,1024]{1,0:T(8,128)(2,1)} %param.27) | copy-start | bytes 786436
  7.3 29.8 %all-gather.7.cloned.1.call-start = ((), (), s32[]{:S(2)}) async-start(), calls=%async_computation.12 | async-start | bytes 1572864 | tf_op jit(solution)/shard_map/all_gather | solution.py:265
  8.0 48.8 %all-gather.9.cloned.1.call-start = ((), (), s32[]{:S(2)}) async-start(), calls=%async_computation.13 | async-start | bytes 1572864 | tf_op jit(solution)/shard_map/all_gather | solution.py:264
  8.8 82.7 %all-gather.11.cloned.1.call-start = ((), (), s32[]{:S(2)}) async-start(), calls=%async_computation.14 | async-start | bytes 3145728 | tf_op jit(solution)/shard_map/all_gather | solution.py:263
  9.5 116.5 %all-gather.13.cloned.1.call-start = ((), (), s32[]{:S(2)}) async-start(), calls=%async_computation.15 | async-start | bytes 3145728 | tf_op jit(solution)/shard_map/all_gather | solution.py:266
  15.6 43.1 %copy-start.57 = (s32[1024,1]{0,1:T(1,128)}, s32[1024,1]{0,1:T(1,128)S(1)}, u32[]{:S(2)}) copy-start(s32[1024,1]{0,1:T(1,128)S(1)} %compare_select_fusion) | copy-start | bytes 12292
  20.1 73.9 %copy-start.53 = (f32[128]{0:T(128)}, f32[128]{0:T(128)S(1)}, u32[]{:S(2)}) copy-start(f32[128]{0:T(128)S(1)} %add_rsqrt_fusion.1) | copy-start | bytes 1540
  25.7 68.4 %copy-start.34 = (f32[2,1,512]{2,1,0:T(1,128)}, f32[2,1,512]{2,1,0:T(1,128)S(1)}, u32[]{:S(2)}) copy-start(f32[2,1,512]{2,1,0:T(1,128)S(1)} %convert_element_type.271) | copy-start | bytes 12292
  30.2 98.0 %copy-start.47 = (f32[2,1,512]{2,1,0:T(1,128)}, f32[2,1,512]{2,1,0:T(1,128)S(1)}, u32[]{:S(2)}) copy-start(f32[2,1,512]{2,1,0:T(1,128)S(1)} %convert_element_type.272) | copy-start | bytes 12292
  30.5 63.6 %copy-start.32 = (f32[128,32]{0,1:T(8,128)}, f32[128,32]{0,1:T(8,128)S(1)}, u32[]{:S(2)}) copy-start(f32[128,32]{0,1:T(8,128)S(1)} %get-tuple-element.45) | copy-start | bytes 49156
  34.9 94.2 %copy-start.37 = (bf16[1024,16]{0,1:T(8,128)(2,1)}, bf16[1024,16]{0,1:T(8,128)(2,1)S(1)}, u32[]{:S(2)}) copy-start(bf16[1024,16]{0,1:T(8,128)(2,1)S(1)} %all_gather.27) | copy-start | bytes 98308
  58.7 36.5 %copy-start.39 = (bf16[128,8,32]{0,2,1:T(8,128)(2,1)}, bf16[128,8,32]{0,2,1:T(8,128)(2,1)S(1)}, u32[]{:S(2)}) copy-start(bf16[128,8,32]{0,2,1:T(8,128)(2,1)S(1)} %get-tuple-element.38) | copy-start | bytes 196612
  58.7 36.5 %copy-start.41 = (bf16[128,8,32]{0,2,1:T(8,128)(2,1)}, bf16[128,8,32]{0,2,1:T(8,128)(2,1)S(1)}, u32[]{:S(2)}) copy-start(bf16[128,8,32]{0,2,1:T(8,128)(2,1)S(1)} %get-tuple-element.39) | copy-start | bytes 196612
  95.4 33.7 %copy-start.45 = (f32[2,8,128]{2,1,0:T(8,128)}, f32[2,8,128]{2,1,0:T(8,128)S(1)}, u32[]{:S(2)}) copy-start(f32[2,8,128]{2,1,0:T(8,128)S(1)} %log_add_fusion) | copy-start | bytes 24580
  96.5 34.7 %copy-start.13 = (bf16[8,64,2,128]{3,1,2,0:T(8,128)(2,1)}, bf16[8,64,2,128]{3,1,2,0:T(8,128)(2,1)S(1)}, u32[]{:S(2)}) copy-start(bf16[8,64,2,128]{3,1,2,0:T(8,128)(2,1)S(1)} %convolution_convert_fusion.9) | copy-start | bytes 786436
  210.7 55.5 %all-to-all-start.2 = ((bf16[16,80,1024]{2,1,0:T(8,128)(2,1)}), bf16[16,80,1024]{2,1,0:T(8,128)(2,1)}, u32[]{:S(2)}, u32[]{:S(2)}) async-start(bf16[16,80,1024]{2,1,0:T(8,128)(2,1)} %get-tuple-element.42), calls=%async_computation.2 | async-start | bytes 5242880 | tf_op jit(solution)/shard_map/all_to_all | solution.py:327
  276.3 63.5 %all-to-all-start.1 = ((bf16[16,80,1024]{2,1,0:T(8,128)(2,1)}), bf16[16,80,1024]{2,1,0:T(8,128)(2,1)}, u32[]{:S(2)}, u32[]{:S(2)}) async-start(bf16[16,80,1024]{2,1,0:T(8,128)(2,1)} %bitcast.202), calls=%async_computation.1 | async-start | bytes 5242880 | tf_op jit(solution)/shard_map/all_to_all | solution.py:309
  339.9 63.7 %all-to-all-start.3 = ((bf16[16,80,1024]{2,1,0:T(8,128)(2,1)}), bf16[16,80,1024]{2,1,0:T(8,128)(2,1)}, u32[]{:S(2)}, u32[]{:S(2)}) async-start(bf16[16,80,1024]{2,1,0:T(8,128)(2,1)} %bitcast.191), calls=%async_computation.3 | async-start | bytes 5242880 | tf_op jit(solution)/shard_map/all_to_all | solution.py:342
  353.4 91.9 %reduce-scatter.13.cloned.1.call-start = ((), (), s32[]{:S(2)}) async-start(), calls=%async_computation.18 | async-start | bytes 1572864 | tf_op jit(solution)/shard_map/reduce_scatter | solution.py:390
  363.4 48.7 %copy-start.51 = (bf16[128,16]{0,1:T(8,128)(2,1)}, bf16[128,16]{0,1:T(8,128)(2,1)S(1)}, u32[]{:S(2)}) copy-start(bf16[128,16]{0,1:T(8,128)(2,1)S(1)} %select_reduce_fusion) | copy-start | bytes 12292
  417.0 51.4 %reduce-scatter.11.cloned.1.call-start = ((), (), s32[]{:S(2)}) async-start(), calls=%async_computation.17 | async-start | bytes 1572864 | tf_op jit(solution)/shard_map/reduce_scatter | solution.py:387
  422.5 80.6 %reduce-scatter.15.cloned.1.call-start = ((), (), s32[]{:S(2)}) async-start(), calls=%async_computation.19 | async-start | bytes 3145728 | tf_op jit(solution)/shard_map/reduce_scatter | solution.py:393
  424.6 113.3 %reduce-scatter.9.cloned.1.call-start = ((), (), s32[]{:S(2)}) async-start(), calls=%async_computation.16 | async-start | bytes 3145728 | tf_op jit(solution)/shard_map/reduce_scatter | solution.py:384
  427.4 133.7 %reduce-scatter.23.cloned.1.call-start = ((), (), s32[]{:S(2)}) async-start(), calls=%async_computation.23 | async-start | bytes 1572864 | tf_op jit(solution)/shard_map/reduce_scatter | solution.py:360
  432.2 152.0 %reduce-scatter.21.cloned.1.call-start = ((), (), s32[]{:S(2)}) async-start(), calls=%async_computation.22 | async-start | bytes 1572864 | tf_op jit(solution)/shard_map/reduce_scatter | solution.py:357
  436.8 170.6 %reduce-scatter.19.cloned.1.call-start = ((), (), s32[]{:S(2)}) async-start(), calls=%async_computation.21 | async-start | bytes 1572864 | tf_op jit(solution)/shard_map/reduce_scatter | solution.py:354
  441.5 96.4 %copy-start.70 = (u32[32]{0:T(128)S(1)}, u32[32]{0:T(128)}, u32[]{:S(2)}) copy-start(u32[32]{0:T(128)} %constant.69) | copy-start | bytes 388
  441.5 178.5 %reduce-scatter.17.cloned.1.call-start = ((), (), s32[]{:S(2)}) async-start(), calls=%async_computation.20 | async-start | bytes 49152 | tf_op jit(solution)/shard_map/reduce_scatter | solution.py:396
  442.4 286.1 %all-reduce.7.cloned.1.call-start = ((), (), s32[]{:S(2)}) async-start(), calls=%async_computation.24 | async-start | bytes 6291456 | tf_op jit(solution)/shard_map/psum | solution.py:407
  537.9 71.8 %copy-start.6 = (bf16[1024,1024]{1,0:T(8,128)(2,1)S(1)}, bf16[1024,1024]{1,0:T(8,128)(2,1)}, u32[]{:S(2)}) copy-start(bf16[1024,1024]{1,0:T(8,128)(2,1)} %all-gather.11.cloned.1.call-done) | copy-start | bytes 6291460
  (55 other events, 221.4 us)
Sparse Core Ops, SparseCore 0:
  9.6 24.2 all-gather.6
  35.5 21.2 all-gather.8
  58.4 33.0 all-gather.10
  92.9 33.0 all-gather.12
  417.1 28.1 reduce-scatter.12
  447.9 20.3 reduce-scatter.10
  471.2 31.8 reduce-scatter.14
  505.9 31.8 reduce-scatter.8
  540.7 20.3 reduce-scatter.22
  563.8 20.3 reduce-scatter.20
  587.0 20.3 reduce-scatter.18
  610.0 9.9 reduce-scatter.16
  623.9 104.5 all-reduce.6
where the time goes:
time: 743 us; the launch traced here: 742 us
  waiting for transfers between devices  416 us (56%)
  blocking collectives  145 us (20%)
  matrix products  62.2 us (8%)
  local copies, waits for them, and re-layouts  35.9 us (5%)
  other arithmetic  34 us (5%)
  starting transfers between devices  33.2 us (4%)
  between operations  15.7 us (2%)
    all_to_all x1, blocking collectives, shards(): lax.all_to_all(send_rows.reshape(expert_count, capacity, model_width), 'e...  63.9 us
    psum x1, blocking collectives, shards(): lax.psum(pieces[5].astype(jnp.bfloat16), 'expert').astype(jnp.float32)  61.4 us
    psum x1, waiting for transfers between devices, shards(): lax.psum(pieces[0].astype(jnp.bfloat16), 'expert').astype(jnp.float32)  45.3 us
    all_to_all x1, waiting for transfers between devices, shards(): lax.all_to_all(to_source(expert_out, owner_count, local_count, capacity),...  43.8 us
    all_to_all x1, waiting for transfers between devices, shards(): lax.all_to_all(grad_send.reshape(expert_count, capacity, model_width), 'e...  42 us
    dot_general x15, matrix products, product(): jnp.einsum(pattern, left_op, right_op, preferred_element_type=jnp.float32)  41.7 us
    all_to_all x1, waiting for transfers between devices, shards(): lax.all_to_all(to_source(grad_owner_rows, owner_count, local_count, capac...  40.2 us
    reduce_scatter x1, waiting for transfers between devices, shards(): lax.psum_scatter(partials[0].astype(jnp.bfloat16), 'dp', scatter_dimensio...  34.8 us
  transfers between devices with their start and end apart: 16, of which 15 were waited for; matrix products, arithmetic and copies ran while one was open for 11% of the time, Pallas kernels for 0%

commit v1 on v0

--- a/solution.py
+++ b/solution.py
@@ -228,19 +228,33 @@
     return (grad_owner_rows.astype(jnp.bfloat16), gate_grad, up_grad, down_grad)
 
 
-def to_owner(arrived, owner_count, local_count):
-    capacity = arrived.shape[1]
-    model_width = arrived.shape[2]
-    shaped = arrived.reshape(owner_count, local_count, capacity, model_width).transpose(1, 0, 2, 3)
-    return shaped.reshape(local_count, owner_count * capacity, model_width)
-
-
-def to_source(owner_rows, owner_count, local_count, capacity):
-    model_width = owner_rows.shape[2]
-    shaped = owner_rows.reshape(local_count, owner_count, capacity, model_width).transpose(
-        1, 0, 2, 3
-    )
-    return shaped.reshape(owner_count * local_count, capacity, model_width)
+def gather_dp(local_part):
+    dp_count = lax.axis_size("dp")
+    if dp_count != 2:
+        return lax.all_gather(local_part, "dp", axis=0, tiled=True)
+    other = lax.ppermute(local_part, "dp", [(0, 1), (1, 0)])
+    first = lax.axis_index("dp") == 0
+    return jnp.concatenate(
+        [jnp.where(first, local_part, other), jnp.where(first, other, local_part)], 0
+    )
+
+
+def scatter_dp(partial, axis):
+    dp_count = lax.axis_size("dp")
+    rounded = partial.astype(jnp.bfloat16)
+    if dp_count != 2:
+        return lax.psum_scatter(rounded, "dp", scatter_dimension=axis, tiled=True).astype(
+            jnp.float32
+        )
+    low, high = jnp.split(rounded, 2, axis)
+    first = lax.axis_index("dp") == 0
+    arrived = lax.ppermute(jnp.where(first, high, low), "dp", [(0, 1), (1, 0)])
+    return jnp.where(first, low, high).astype(jnp.float32) + arrived.astype(jnp.float32)
+
+
+def two_parts(values):
+    high = lax.reduce_precision(values, 8, 7)
+    return (high.astype(jnp.bfloat16), (values - high).astype(jnp.bfloat16))
 
 
 def shards(
@@ -259,110 +273,112 @@
     down_weight,
     cotangent,
 ):
-    gathered = (
-        lax.all_gather(query_weight, "dp", axis=0, tiled=True),
-        lax.all_gather(key_projection_weight, "dp", axis=0, tiled=True),
-        lax.all_gather(value_projection_weight, "dp", axis=0, tiled=True),
-        lax.all_gather(out_weight, "dp", axis=0, tiled=True),
-        lax.all_gather(router_weight, "dp", axis=0, tiled=True),
-        lax.all_gather(first_gain, "dp", axis=0, tiled=True),
-        lax.all_gather(second_gain, "dp", axis=0, tiled=True),
-    )
-    query_mat, key_matrix, value_matrix, out_mat, router_mat, gain_first, gain_second = gathered
-    token_rows = tokens.shape[0]
-    model_width = tokens.shape[1]
+    token_rows, model_width = tokens.shape
     top_count = routes.shape[1]
-    expert_count = router_mat.shape[1]
+    expert_count = router_weight.shape[1]
     owner_count = lax.axis_size("expert")
     local_count = gate_weight.shape[0]
+    key_width = key_projection_weight.shape[1]
+    query_width = query_weight.shape[1]
     capacity = 5 * token_rows * top_count // (4 * expert_count)
+    row_part = router_weight.shape[0]
+
+    small = jnp.concatenate(
+        [router_weight, first_gain[:, None], second_gain[:, None]], 1
+    )
+    small_mat = gather_dp(small)
+    router_mat = small_mat[:, :expert_count]
+    gain_first = small_mat[:, expert_count]
+    gain_second = small_mat[:, expert_count + 1]
+    query_mat = gather_dp(query_weight)
+    key_matrix = gather_dp(key_projection_weight)
+    value_matrix = gather_dp(value_projection_weight)
+    out_mat = gather_dp(out_weight)
+
+    routes_all = lax.all_gather(routes, "expert")
+    cotangent_all = lax.all_gather(cotangent, "expert")
+
+    mine = lax.axis_index("expert") * local_count + jnp.arange(local_count, dtype=jnp.int32)
+    hit = jnp.any(routes_all[None] == mine[:, None, None, None], -1)
+    before = (
+        jnp.arange(token_rows)[:, None] < jnp.arange(token_rows)[None, :]
+    ).astype(jnp.bfloat16)
+    rank = product("lst,tu->lsu", hit.astype(jnp.bfloat16), before).astype(jnp.int32)
+    slot = jnp.where(hit, rank, -1)
+    picked = slot[:, :, None, :] == jnp.arange(capacity, dtype=jnp.int32)[None, None, :, None]
+    pick = picked.astype(jnp.bfloat16)
+
+    def rows_of(gathered):
+        rows = product("lsct,std->lscd", pick, gathered)
+        return rows.reshape(local_count, owner_count * capacity, model_width)
+
+    def tokens_of(rows):
+        shaped = rows.reshape(local_count, owner_count, capacity, rows.shape[-1])
+        return product("lsct,lscd->std", pick, shaped).astype(jnp.bfloat16)
+
     hidden, saved = mixer_forward(
         tokens, segments, gain_first, query_mat, key_matrix, value_matrix, out_mat
     )
     normed_second, factor_second, expert_input = normalize(hidden, gain_second)
+    input_all = lax.all_gather(expert_input, "expert")
     route_prob, chosen_hot = route_weights(expert_input, router_mat, routes)
-    flat_routes = routes.reshape(-1)
-    route_hot = (flat_routes[:, None] == jnp.arange(expert_count, dtype=jnp.int32)[None, :]).astype(
-        jnp.int32
-    )
-    slot_of = jnp.sum(route_hot * jnp.cumsum(route_hot, 0), 1) - 1
-    target = flat_routes * capacity + slot_of
-    entries = (
-        jnp.full((expert_count * capacity,), -1, jnp.int32)
-        .at[target]
-        .set(jnp.arange(token_rows * top_count, dtype=jnp.int32))
-    )
-    live_slot = entries >= 0
-    source = jnp.maximum(entries, 0)
-    send_rows = jnp.where(
-        live_slot[:, None], expert_input[source // top_count], jnp.zeros((), jnp.bfloat16)
-    )
-    arrived = lax.all_to_all(
-        send_rows.reshape(expert_count, capacity, model_width),
+    dense_prob = jnp.sum(chosen_hot * route_prob[:, :, None], 1)
+    prob_all = lax.all_gather(dense_prob, "expert")
+
+    column = jnp.arange(expert_count, dtype=jnp.int32)
+    my_column = (mine[:, None] == column[None, :]).astype(jnp.float32)
+    my_prob = jnp.sum(prob_all[None] * my_column[:, None, None, :], -1)
+    row_prob = jnp.sum(jnp.where(picked, my_prob[:, :, None, :], 0.0), -1).reshape(
+        local_count, owner_count * capacity, 1
+    )
+
+    owner_rows = rows_of(input_all).astype(jnp.bfloat16)
+    cotangent_rows = rows_of(cotangent_all).astype(jnp.bfloat16).astype(jnp.float32)
+    expert_out, kept_acts = expert_forward(owner_rows, gate_weight, up_weight, down_weight)
+    expert_out = expert_out.astype(jnp.float32)
+    weighted = (row_prob * expert_out).astype(jnp.bfloat16)
+    row_grad_prob = jnp.sum(expert_out * cotangent_rows, -1).reshape(
+        local_count, owner_count, capacity
+    )
+    token_grad_prob = jnp.sum(jnp.where(picked, row_grad_prob[..., None], 0.0), 2)
+    dense_grad_prob = jnp.sum(
+        token_grad_prob[..., None] * my_column[:, None, None, :], 0
+    )
+    high_part, low_part = two_parts(dense_grad_prob)
+    forward_send = jnp.concatenate([tokens_of(weighted), high_part, low_part], -1)
+    forward_sum = lax.psum_scatter(
+        forward_send.reshape(owner_count * token_rows, -1),
         "expert",
-        split_axis=0,
-        concat_axis=0,
+        scatter_dimension=0,
         tiled=True,
-    )
-    owner_rows = to_owner(arrived, owner_count, local_count)
-    expert_out, kept_acts = expert_forward(owner_rows, gate_weight, up_weight, down_weight)
-    returned = lax.all_to_all(
-        to_source(expert_out, owner_count, local_count, capacity),
+    ).astype(jnp.float32)
+    output = (hidden + forward_sum[:, :model_width]).astype(jnp.bfloat16)
+    dense_back = (
+        forward_sum[:, model_width : model_width + expert_count]
+        + forward_sum[:, model_width + expert_count :]
+    )
+    grad_prob = jnp.sum(chosen_hot * dense_back[:, None, :], -1)
+    grad_output = cotangent.astype(jnp.float32)
+
+    grad_rows = (row_prob * cotangent_rows).astype(jnp.bfloat16)
+    grad_owner_rows, gate_grad, up_grad, down_grad = expert_backward(
+        grad_rows, owner_rows, kept_acts, gate_weight, up_weight, down_weight
+    )
+    backward_sum = lax.psum_scatter(
+        tokens_of(grad_owner_rows).reshape(owner_count * token_rows, -1),
         "expert",
-        split_axis=0,
-        concat_axis=0,
+        scatter_dimension=0,
         tiled=True,
     )
-    out_rows = returned.reshape(expert_count * capacity, model_width)[target]
-    out_rows = out_rows.reshape(token_rows, top_count, model_width).astype(jnp.float32)
-    output = (hidden + jnp.sum(route_prob[:, :, None] * out_rows, 1)).astype(jnp.bfloat16)
-    grad_output = cotangent.astype(jnp.float32)
-    grad_pairs = (
-        (route_prob[:, :, None] * grad_output[:, None, :])
-        .astype(jnp.bfloat16)
-        .reshape(token_rows * top_count, model_width)
-    )
-    grad_prob = jnp.sum(out_rows * grad_output[:, None, :], -1)
-    grad_send = jnp.where(live_slot[:, None], grad_pairs[source], jnp.zeros((), jnp.bfloat16))
-    grad_arrived = lax.all_to_all(
-        grad_send.reshape(expert_count, capacity, model_width),
-        "expert",
-        split_axis=0,
-        concat_axis=0,
-        tiled=True,
-    )
-    grad_owner_rows, gate_grad, up_grad, down_grad = expert_backward(
-        to_owner(grad_arrived, owner_count, local_count),
-        owner_rows,
-        kept_acts,
-        gate_weight,
-        up_weight,
-        down_weight,
-    )
-    grad_back = lax.all_to_all(
-        to_source(grad_owner_rows, owner_count, local_count, capacity),
-        "expert",
-        split_axis=0,
-        concat_axis=0,
-        tiled=True,
-    )
-    grad_pair_rows = grad_back.reshape(expert_count * capacity, model_width)[target]
-    grad_expert_input = jnp.sum(
-        grad_pair_rows.reshape(token_rows, top_count, model_width).astype(jnp.float32), 1
-    )
     expert_shares = (
-        lax.psum_scatter(
-            gate_grad.astype(jnp.bfloat16), "dp", scatter_dimension=1, tiled=True
-        ).astype(jnp.float32),
-        lax.psum_scatter(
-            up_grad.astype(jnp.bfloat16), "dp", scatter_dimension=1, tiled=True
-        ).astype(jnp.float32),
-        lax.psum_scatter(
-            down_grad.astype(jnp.bfloat16), "dp", scatter_dimension=2, tiled=True
-        ).astype(jnp.float32),
+        scatter_dp(gate_grad, 1),
+        scatter_dp(up_grad, 1),
+        scatter_dp(down_grad, 2),
     )
     router_grad = route_back(route_prob, grad_prob, chosen_hot)
-    grad_expert_input = grad_expert_input + matrix_multiply(router_grad, router_mat.T)
+    grad_expert_input = backward_sum.astype(jnp.float32) + matrix_multiply(
+        router_grad, router_mat.T
+    )
     router_wgrad = matrix_multiply(expert_input.T, router_grad)
     grad_normed, second_gain_grad = normalize_back(
         grad_expert_input, normed_second, factor_second, gain_second
@@ -371,57 +387,42 @@
     grad_tokens, first_gain_grad, query_wgrad, key_wgrad, value_wgrad, out_wgrad = mixer_backward(
         grad_hidden, saved, gain_first, query_mat, key_matrix, value_matrix, out_mat
     )
-    partials = (
-        query_wgrad,
-        key_wgrad,
-        value_wgrad,
-        out_wgrad,
-        router_wgrad,
-        first_gain_grad,
-        second_gain_grad,
-    )
-    pieces = (
-        lax.psum_scatter(
-            partials[0].astype(jnp.bfloat16), "dp", scatter_dimension=0, tiled=True
-        ).astype(jnp.float32),
-        lax.psum_scatter(
-            partials[1].astype(jnp.bfloat16), "dp", scatter_dimension=0, tiled=True
-        ).astype(jnp.float32),
-        lax.psum_scatter(
-            partials[2].astype(jnp.bfloat16), "dp", scatter_dimension=0, tiled=True
-        ).astype(jnp.float32),
-        lax.psum_scatter(
-            partials[3].astype(jnp.bfloat16), "dp", scatter_dimension=0, tiled=True
-        ).astype(jnp.float32),
-        lax.psum_scatter(
-            partials[4].astype(jnp.bfloat16), "dp", scatter_dimension=0, tiled=True
-        ).astype(jnp.float32),
-        lax.psum_scatter(
-            partials[5].astype(jnp.bfloat16), "dp", scatter_dimension=0, tiled=True
-        ).astype(jnp.float32),
-        lax.psum_scatter(
-            partials[6].astype(jnp.bfloat16), "dp", scatter_dimension=0, tiled=True
-        ).astype(jnp.float32),
-    )
-    shares = (
-        lax.psum(pieces[0].astype(jnp.bfloat16), "expert").astype(jnp.float32),
-        lax.psum(pieces[1].astype(jnp.bfloat16), "expert").astype(jnp.float32),
-        lax.psum(pieces[2].astype(jnp.bfloat16), "expert").astype(jnp.float32),
-        lax.psum(pieces[3].astype(jnp.bfloat16), "expert").astype(jnp.float32),
-        lax.psum(pieces[4].astype(jnp.bfloat16), "expert").astype(jnp.float32),
-        lax.psum(pieces[5].astype(jnp.bfloat16), "expert").astype(jnp.float32),
-        lax.psum(pieces[6].astype(jnp.bfloat16), "expert").astype(jnp.float32),
-    )
-    query_share, key_share, value_share, out_share, router_share, first_share, second_share = shares
+
+    def total(partial):
+        piece = lax.psum_scatter(
+            partial.astype(jnp.bfloat16), ("dp", "expert"), scatter_dimension=0, tiled=True
+        )
+        return lax.all_gather(piece, "expert", axis=0, tiled=True)
+
+    out_share = total(out_wgrad).astype(jnp.float32)
+    joined = total(
+        jnp.concatenate(
+            [
+                query_wgrad,
+                key_wgrad,
+                value_wgrad,
+                router_wgrad,
+                first_gain_grad[:, None],
+                second_gain_grad[:, None],
+            ],
+            1,
+        )
+    ).astype(jnp.float32)
+    cuts = []
+    start = 0
+    for width in (query_width, key_width, key_width, expert_count, 1, 1):
+        cuts.append(joined[:, start : start + width])
+        start += width
+    query_share, key_share, value_share, router_share, first_share, second_share = cuts
     return (
         output,
         grad_tokens,
-        first_share,
+        first_share.reshape(row_part),
         query_share,
         key_share,
         value_share,
         out_share,
-        second_share,
+        second_share.reshape(row_part),
         router_share,
         expert_shares[0],
         expert_shares[1],

time: 743 us -> 701 us (0.943)
  blocking collectives: 145 us -> 40.7 us
  waiting for transfers between devices: 416 us -> 494 us
  starting transfers between devices: 33.2 us -> 11.4 us
  local copies, waits for them, and re-layouts: 35.9 us -> 44.7 us
    reduce_scatter x8 -> x4, waiting for transfers between devices: 162 us -> 380 us  [the longest x2 246 us: total(): lax.psum_scatter(partial.astype(jnp.bfloat16), ('dp', 'expert'), scatter_...]
    all_to_all x3 -> x0, waiting for transfers between devices: 126 us -> none  [the longest x1 43.8 us: shards(): lax.all_to_all(to_source(expert_out, owner_count, local_count, capacity),...]
    ppermute x0 -> x8, waiting for transfers between devices: none -> 72.5 us  [the longest x5 50.3 us: gather_dp(): other = lax.ppermute(local_part, 'dp', [(0, 1), (1, 0)])]
    all_to_all x1 -> x0, blocking collectives: 63.9 us -> none  [shards(): lax.all_to_all(send_rows.reshape(expert_count, capacity, model_width), 'e...]
    psum x1 -> x0, blocking collectives: 61.4 us -> none  [shards(): lax.psum(pieces[5].astype(jnp.bfloat16), 'expert').astype(jnp.float32)]
    psum x1 -> x0, waiting for transfers between devices: 45.3 us -> none  [shards(): lax.psum(pieces[0].astype(jnp.bfloat16), 'expert').astype(jnp.float32)]
    all_gather x4, waiting for transfers between devices: 80.3 us -> 40.5 us  [the longest x2 40.5 us: total(): return lax.all_gather(piece, 'expert', axis=0, tiled=True)]
    all_to_all x3 -> x0, starting transfers between devices: 32.2 us -> none  [the longest x1 13.5 us: shards(): lax.all_to_all(to_source(grad_owner_rows, owner_count, local_count, capac...]
  transfers between devices with their start and end apart: 16 -> 16, of which waited for: 15 -> 13; matrix products, arithmetic and copies ran while one was open for 11% -> 13% of each run, Pallas kernels for 0% -> 0%
where the time goes in v1:
time: 701 us; the launch traced here: 699 us
  waiting for transfers between devices  494 us (70%)
  matrix products  60.7 us (9%)
  local copies, waits for them, and re-layouts  44.7 us (6%)
  blocking collectives  40.7 us (6%)
  other arithmetic  32.8 us (5%)
  between operations  15.3 us (2%)
  starting transfers between devices  11.4 us (2%)
    reduce_scatter x2, waiting for transfers between devices, total(): lax.psum_scatter(partial.astype(jnp.bfloat16), ('dp', 'expert'), scatter_...  246 us
    reduce_scatter x1, waiting for transfers between devices, shards(): lax.psum_scatter(tokens_of(grad_owner_rows).reshape(owner_count * token_r...  74.5 us
    reduce_scatter x1, waiting for transfers between devices, shards(): lax.psum_scatter(forward_send.reshape(owner_count * token_rows, -1), 'exp...  59.4 us
    ppermute x5, waiting for transfers between devices, gather_dp(): other = lax.ppermute(local_part, 'dp', [(0, 1), (1, 0)])  50.3 us
    dot_general x20, matrix products, product(): jnp.einsum(pattern, left_op, right_op, preferred_element_type=jnp.float32)  43.5 us
    all_gather x2, waiting for transfers between devices, total(): return lax.all_gather(piece, 'expert', axis=0, tiled=True)  40.5 us
    ppermute x3, waiting for transfers between devices, scatter_dp(): arrived = lax.ppermute(jnp.where(first, high, low), 'dp', [(0, 1), (1, 0)])  22.2 us
    all_gather x1, blocking collectives, shards(): routes_all = lax.all_gather(routes, 'expert')  21.9 us
  transfers between devices with their start and end apart: 16, of which 13 were waited for; matrix products, arithmetic and copies ran while one was open for 13% of the time, Pallas kernels for 0%

profile of v1, /device:TPU:0, one launch (start us, length us, event | category | flops | bytes accessed | tf_op | source)
XLA Modules:
  0.0 699.4 jit_solution(3687725492733086078)
XLA Ops:
  10.1 3.1 collective-permute-start
  21.3 6.9 collective-permute-done.2
  28.1 11.2 %collective-permute-done.1 = bf16[512,512]{1,0:T(8,128)(2,1)S(1)} collective-permute-done((bf16[512,512]{1,0:T(8,128)(2,1)}, bf16[512,512]{1,0:T(8,128)(2,1)S(1)}, u32[]{:S(2)}, u32[]{:S(2)}) %collective-permute-start.1) | collective-permute-done | bytes 524320 | tf_op jit(solution)/shard_map/ppermute | solution.py:235
  39.4 2.2 broadcast_select_fusion.8
  46.4 15.6 %collective-permute-done.3 = bf16[512,1024]{1,0:T(8,128)(2,1)} collective-permute-done((bf16[512,1024]{1,0:T(8,128)(2,1)}, bf16[512,1024]{1,0:T(8,128)(2,1)}, u32[]{:S(2)}, u32[]{:S(2)}) %collective-permute-start.3) | collective-permute-done | bytes 1048608 | tf_op jit(solution)/shard_map/ppermute | solution.py:235
  66.4 16.6 %collective-permute-done.4 = bf16[512,1024]{1,0:T(8,128)(2,1)} collective-permute-done((bf16[512,1024]{1,0:T(8,128)(2,1)}, bf16[512,1024]{1,0:T(8,128)(2,1)}, u32[]{:S(2)}, u32[]{:S(2)}) %collective-permute-start.4) | collective-permute-done | bytes 1048608 | tf_op jit(solution)/shard_map/ppermute | solution.py:235
  86.9 21.9 %all-gather = s32[2048,8]{0,1:T(8,128)S(1)} all-gather(s32[128,8]{0,1:T(8,128)S(1)} %copy-done.58), channel_id=2, replica_groups=mesh['dp'=2,'expert'=16] {'expert'}, dimensions={0}, use_global_device_ids=true | all-gather | bytes 69632 | tf_op jit(solution)/shard_map/all_gather | solution.py:298
  111.9 18.8 %all-gather.1 = f32[2048,16]{0,1:T(8,128)S(1)} all-gather(f32[128,16]{0,1:T(8,128)S(1)} %select_reduce_fusion.4), channel_id=3, replica_groups=mesh['dp'=2,'expert'=16] {'expert'}, dimensions={0}, use_global_device_ids=true | all-gather | bytes 139264 | tf_op jit(solution)/shard_map/all_gather | solution.py:326
  133.6 6.4 bitcast_convert_fusion
  140.1 3.1 convolution_convert_fusion.4
  145.3 3.4 multiply_convert_fusion.3
  148.7 3.2 fusion.1
  153.9 4.9 fusion.2
  158.8 3.4 convolution_convert_fusion.2
  162.2 7.9 %concatenate.74 = bf16[16,128,1056]{2,1,0:T(8,128)(2,1)} concatenate(bf16[16,128,1024]{2,1,0:T(8,128)(2,1)} %convolution_convert_fusion.2, bf16[16,128,16]{2,1,0:T(8,128)(2,1)} %get-tuple-element.107, bf16[16,128,16]{2,1,0:T(8,128)(2,1)} %get-tuple-element.106), dimensions={2} | concatenate | bytes 8650752 | tf_op jit(solution)/shard_map/concatenate | solution.py:348
  170.4 6.9 multiply_convert_fusion.1
  181.0 3.3 convolution_convert_fusion.1
  184.5 59.4 %reduce-scatter.7.cloned.1.call-done = bf16[128,1056]{1,0:T(8,128)(2,1)} async-done(((bf16[2048,1056]{1,0:T(8,128)(2,1)}), bf16[128,1056]{1,0:T(8,128)(2,1)}) %reduce-scatter.7.cloned.1.call-update) | async-done | bytes 270352 | tf_op jit(solution)/shard_map/reduce_scatter | solution.py:349
  245.2 74.5 %reduce-scatter.9.cloned.1.call-done = bf16[128,1024]{1,0:T(8,128)(2,1)} async-done(((bf16[2048,1024]{1,0:T(8,128)(2,1)}), bf16[128,1024]{1,0:T(8,128)(2,1)}) %reduce-scatter.9.cloned.1.call-update) | async-done | bytes 262160 | tf_op jit(solution)/shard_map/reduce_scatter | solution.py:367
  323.6 2.0 convolution_convert_fusion.6
  326.0 2.4 fusion.25
  337.1 14.7 %concatenate.77 = bf16[1024,2066]{0,1:T(8,128)(2,1)} concatenate(bf16[1024,1024]{0,1:T(8,128)(2,1)S(1)} %convolution_convert_fusion.5, bf16[1024,512]{0,1:T(8,128)(2,1)S(1)} %convolution_convert_fusion.8, bf16[1024,512]{0,1:T(8,128)(2,1)} %convolution_convert_fusion.7, bf16[1024,16]{0,1:T(8,128)(2,1)S(1)} %convolution_convert_fusion.14, bf16[1024,1]{0,1:T(2,128)(2,1)S(1)} %broadcast_in_dim.63, ...), dimensions={1} | concatenate | bytes 8462336 | tf_op jit(solution)/shard_map/concatenate | solution.py:399
  351.8 6.3 copy.114
  358.2 105.1 %reduce-scatter.11.cloned.1.call-done = bf16[32,1024]{1,0:T(8,128)(2,1)} async-done(((bf16[1024,1024]{1,0:T(8,128)(2,1)}), bf16[32,1024]{1,0:T(8,128)(2,1)}) %reduce-scatter.11.cloned.1.call-update) | async-done | bytes 65552 | tf_op jit(solution)/shard_map/reduce_scatter | solution.py:392
  463.3 141.1 %reduce-scatter.13.cloned.1.call-done = bf16[32,2066]{1,0:T(8,128)(2,1)} async-done(((bf16[1024,2066]{1,0:T(8,128)(2,1)}), bf16[32,2066]{1,0:T(8,128)(2,1)}) %reduce-scatter.13.cloned.1.call-update) | async-done | bytes 132240 | tf_op jit(solution)/shard_map/reduce_scatter | solution.py:392
  604.5 3.4 fusion.10
  614.7 8.1 %collective-permute-done.7 = bf16[1,512,512]{2,1,0:T(8,128)(2,1)S(1)} collective-permute-done((bf16[1,512,512]{2,1,0:T(8,128)(2,1)S(1)}, bf16[1,512,512]{2,1,0:T(8,128)(2,1)S(1)}, u32[]{:S(2)}, u32[]{:S(2)}) %collective-permute-start.7) | collective-permute-done | bytes 524320 | tf_op jit(solution)/shard_map/ppermute | solution.py:251
  624.0 9.6 %collective-permute-done.6 = bf16[1,512,512]{2,1,0:T(8,128)(2,1)S(1)} collective-permute-done((bf16[1,512,512]{2,1,0:T(8,128)(2,1)S(1)}, bf16[1,512,512]{2,1,0:T(8,128)(2,1)S(1)}, u32[]{:S(2)}, u32[]{:S(2)}) %collective-permute-start.6) | collective-permute-done | bytes 524320 | tf_op jit(solution)/shard_map/ppermute | solution.py:251
  634.8 4.4 collective-permute-done.5
  641.5 2.8 convert_element_type.376
  644.3 40.4 %all-gather.9.cloned.1.call-done = bf16[512,2066]{1,0:T(8,128)(2,1)} async-done(((bf16[32,2066]{1,0:T(8,128)(2,1)}), bf16[512,2066]{1,0:T(8,128)(2,1)}) %all-gather.9.cloned.1.call-update) | async-done | bytes 2115600 | tf_op jit(solution)/shard_map/all_gather | solution.py:395
  686.4 2.1 convert_element_type.374
  (276 shorter events, 69.0 us)
Async XLA Ops:
  7.2 141.5 %copy-start = (bf16[1,512,1024]{2,1,0:T(8,128)(2,1)S(1)}, bf16[1,512,1024]{2,1,0:T(8,128)(2,1)}, u32[]{:S(2)}) copy-start(bf16[1,512,1024]{2,1,0:T(8,128)(2,1)} %param.26) | copy-start | bytes 3145732
  7.2 35.4 %copy-start.4 = (bf16[128,1024]{1,0:T(8,128)(2,1)S(1)}, bf16[128,1024]{1,0:T(8,128)(2,1)}, u32[]{:S(2)}) copy-start(bf16[128,1024]{1,0:T(8,128)(2,1)} %param.14) | copy-start | bytes 786436
  7.2 126.4 %all-gather.15.cloned.1.call-start = ((), (), s32[]{:S(2)}) async-start(), calls=%async_computation.10 | async-start | bytes 4456448 | tf_op jit(solution)/shard_map/all_gather | solution.py:299
  7.9 132.1 %all-gather.13.cloned.1.call-start = ((), (), s32[]{:S(2)}) async-start(), calls=%async_computation.9 | async-start | bytes 4456448 | tf_op jit(solution)/shard_map/all_gather | solution.py:323
  10.1 9.8 %collective-permute-start = (bf16[512,18]{0,1:T(8,128)(2,1)S(1)}, bf16[512,18]{0,1:T(8,128)(2,1)S(1)}, u32[]{:S(2)}, u32[]{:S(2)}) collective-permute-start(bf16[512,18]{0,1:T(8,128)(2,1)S(1)} %pad_maximum_fusion.26), channel_id=1, source_target_pairs={{0,16},{16,0},{1,17},{17,1},{2,18},{18,2},{3,19},{19,3},{4,20},{20... | collective-permute-start | bytes 55304 | tf_op jit(solution)/shard_map/ppermute | solution.py:235
  13.1 15.0 %collective-permute-start.2 = (bf16[512,512]{1,0:T(8,128)(2,1)}, bf16[512,512]{1,0:T(8,128)(2,1)S(1)}, u32[]{:S(2)}, u32[]{:S(2)}) collective-permute-start(bf16[512,512]{1,0:T(8,128)(2,1)} %param.19), channel_id=1, source_target_pairs={{0,16},{16,0},{1,17},{17,1},{2,18},{18,2},{3,19},{19,3},{4,20},{20... | collective-permute-start | bytes 1572872 | tf_op jit(solution)/shard_map/ppermute | solution.py:235
  13.2 26.2 %collective-permute-start.1 = (bf16[512,512]{1,0:T(8,128)(2,1)}, bf16[512,512]{1,0:T(8,128)(2,1)S(1)}, u32[]{:S(2)}, u32[]{:S(2)}) collective-permute-start(bf16[512,512]{1,0:T(8,128)(2,1)} %param.20), channel_id=1, source_target_pairs={{0,16},{16,0},{1,17},{17,1},{2,18},{18,2},{3,19},{19,3},{4,20},{20... | collective-permute-start | bytes 1572872 | tf_op jit(solution)/shard_map/ppermute | solution.py:235
  15.2 46.8 %collective-permute-start.3 = (bf16[512,1024]{1,0:T(8,128)(2,1)}, bf16[512,1024]{1,0:T(8,128)(2,1)}, u32[]{:S(2)}, u32[]{:S(2)}) collective-permute-start(bf16[512,1024]{1,0:T(8,128)(2,1)} %param.18), channel_id=1, source_target_pairs={{0,16},{16,0},{1,17},{17,1},{2,18},{18,2},{3,19},{19,3},{4,20},{20... | collective-permute-start | bytes 3145736 | tf_op jit(solution)/shard_map/ppermute | solution.py:235
  15.2 67.8 %collective-permute-start.4 = (bf16[512,1024]{1,0:T(8,128)(2,1)}, bf16[512,1024]{1,0:T(8,128)(2,1)}, u32[]{:S(2)}, u32[]{:S(2)}) collective-permute-start(bf16[512,1024]{1,0:T(8,128)(2,1)} %param.21), channel_id=1, source_target_pairs={{0,16},{16,0},{1,17},{17,1},{2,18},{18,2},{3,19},{19,3},{4,20},{20... | collective-permute-start | bytes 3145736 | tf_op jit(solution)/shard_map/ppermute | solution.py:235
  19.9 43.5 %copy-start.71 = (f32[128]{0:T(128)}, f32[128]{0:T(128)S(1)}, u32[]{:S(2)}) copy-start(f32[128]{0:T(128)S(1)} %add_rsqrt_fusion.1) | copy-start | bytes 1540
  21.3 42.2 %copy-start.56 = (f32[1024,1]{0,1:T(1,128)}, f32[1024,1]{0,1:T(1,128)S(1)}, u32[]{:S(2)}) copy-start(f32[1024,1]{0,1:T(1,128)S(1)} %get-tuple-element.103) | copy-start | bytes 12292
  86.8 157.0 %reduce-scatter.7.cloned.1.call-start = ((), (), s32[]{:S(2)}) async-start(), calls=%async_computation.4 | async-start | bytes 5013504 | tf_op jit(solution)/shard_map/reduce_scatter | solution.py:349
  170.1 149.5 %reduce-scatter.9.cloned.1.call-start = ((), (), s32[]{:S(2)}) async-start(), calls=%async_computation.5 | async-start | bytes 4456448 | tf_op jit(solution)/shard_map/reduce_scatter | solution.py:367
  184.3 60.7 %copy-start.59 = (s32[128,8]{0,1:T(8,128)S(1)}, s32[128,8]{0,1:T(8,128)}, u32[]{:S(2)}) copy-start(s32[128,8]{0,1:T(8,128)} %param.16) | copy-start | bytes 12292
  184.3 60.8 %copy-start.52 = (f32[128,8]{0,1:T(8,128)S(1)}, f32[128,8]{0,1:T(8,128)}, u32[]{:S(2)}) copy-start(f32[128,8]{0,1:T(8,128)} %copy-done.51) | copy-start | bytes 12292
  184.3 60.8 %copy-start.67 = (f32[128]{0:T(128)S(1)}, f32[128]{0:T(128)}, u32[]{:S(2)}) copy-start(f32[128]{0:T(128)} %copy-done.66) | copy-start | bytes 1540
  184.3 60.8 %copy-start.70 = (f32[128]{0:T(128)S(1)}, f32[128]{0:T(128)}, u32[]{:S(2)}) copy-start(f32[128]{0:T(128)} %copy-done.69) | copy-start | bytes 1540
  184.3 135.4 %copy-start.42 = (bf16[512,18]{0,1:T(8,128)(2,1)S(1)}, bf16[512,18]{0,1:T(8,128)(2,1)}, u32[]{:S(2)}) copy-start(bf16[512,18]{0,1:T(8,128)(2,1)} %copy-done.40) | copy-start | bytes 55300
  184.3 135.3 %copy-start.45 = (bf16[512,18]{0,1:T(8,128)(2,1)S(1)}, bf16[512,18]{0,1:T(8,128)(2,1)}, u32[]{:S(2)}) copy-start(bf16[512,18]{0,1:T(8,128)(2,1)} %copy-done.43) | copy-start | bytes 55300
  184.4 135.3 %copy-start.61 = (f32[1024,1]{0,1:T(1,128)S(1)}, f32[1024,1]{0,1:T(1,128)}, u32[]{:S(2)}) copy-start(f32[1024,1]{0,1:T(1,128)} %get-tuple-element.102) | copy-start | bytes 12292
  184.4 135.3 %copy-start.74 = (f32[128]{0:T(128)S(1)}, f32[128]{0:T(128)}, u32[]{:S(2)}) copy-start(f32[128]{0:T(128)} %copy-done.73) | copy-start | bytes 1540
  184.4 137.2 %copy-start.25 = (bf16[128,1024]{1,0:T(8,128)(2,1)S(1)}, bf16[128,1024]{1,0:T(8,128)(2,1)}, u32[]{:S(2)}) copy-start(bf16[128,1024]{1,0:T(8,128)(2,1)} %param.27) | copy-start | bytes 786436
  184.4 278.9 %reduce-scatter.11.cloned.1.call-start = ((), (), s32[]{:S(2)}) async-start(), calls=%async_computation.7 | async-start | bytes 2162688 | tf_op jit(solution)/shard_map/reduce_scatter | solution.py:392
  244.9 76.8 %copy-start.8 = (f32[128,1056]{1,0:T(8,128)}, f32[128,1056]{1,0:T(8,128)S(1)}, u32[]{:S(2)}) copy-start(f32[128,1056]{1,0:T(8,128)S(1)} %convert_element_type.353) | copy-start | bytes 1622020
  245.2 80.5 %copy-start.62 = (bf16[128,16]{0,1:T(8,128)(2,1)}, bf16[128,16]{0,1:T(8,128)(2,1)S(1)}, u32[]{:S(2)}) copy-start(bf16[128,16]{0,1:T(8,128)(2,1)S(1)} %select_reduce_fusion.2) | copy-start | bytes 12292
  325.7 278.8 %reduce-scatter.13.cloned.1.call-start = ((), (), s32[]{:S(2)}) async-start(), calls=%async_computation.11 | async-start | bytes 4595712 | tf_op jit(solution)/shard_map/reduce_scatter | solution.py:392
  358.1 246.4 %copy-start.14 = (bf16[1280,512]{1,0:T(8,128)(2,1)S(1)}, bf16[1280,512]{1,0:T(8,128)(2,1)}, u32[]{:S(2)}) copy-start(bf16[1280,512]{1,0:T(8,128)(2,1)} %copy-done.13) | copy-start | bytes 3932164
  358.1 283.4 %all-gather.11.cloned.1.call-start = ((), (), s32[]{:S(2)}) async-start(), calls=%async_computation.8 | async-start | bytes 1114112 | tf_op jit(solution)/shard_map/all_gather | solution.py:395
  463.3 221.4 %all-gather.9.cloned.1.call-start = ((), (), s32[]{:S(2)}) async-start(), calls=%async_computation.6 | async-start | bytes 2367488 | tf_op jit(solution)/shard_map/all_gather | solution.py:395
  608.0 14.9 %collective-permute-start.7 = (bf16[1,512,512]{2,1,0:T(8,128)(2,1)S(1)}, bf16[1,512,512]{2,1,0:T(8,128)(2,1)S(1)}, u32[]{:S(2)}, u32[]{:S(2)}) collective-permute-start(bf16[1,512,512]{2,1,0:T(8,128)(2,1)S(1)} %broadcast_select_fusion.4), channel_id=1, source_target_pairs={{0,16},{16,0},{1,17},{17,1},{2,18},{18,2},{3,19},{19,3},{4,20},{20... | collective-permute-start | bytes 1572872 | tf_op jit(solution)/shard_map/ppermute | solution.py:251
  611.0 22.7 %collective-permute-start.6 = (bf16[1,512,512]{2,1,0:T(8,128)(2,1)S(1)}, bf16[1,512,512]{2,1,0:T(8,128)(2,1)S(1)}, u32[]{:S(2)}, u32[]{:S(2)}) collective-permute-start(bf16[1,512,512]{2,1,0:T(8,128)(2,1)S(1)} %broadcast_select_fusion.5), channel_id=1, source_target_pairs={{0,16},{16,0},{1,17},{17,1},{2,18},{18,2},{3,19},{19,3},{4,20},{20... | collective-permute-start | bytes 1572872 | tf_op jit(solution)/shard_map/ppermute | solution.py:251
  613.4 25.8 %collective-permute-start.5 = (bf16[1,512,512]{2,1,0:T(8,128)(2,1)S(1)}, bf16[1,512,512]{2,1,0:T(8,128)(2,1)S(1)}, u32[]{:S(2)}, u32[]{:S(2)}) collective-permute-start(bf16[1,512,512]{2,1,0:T(8,128)(2,1)S(1)} %broadcast_select_fusion.6), channel_id=1, source_target_pairs={{0,16},{16,0},{1,17},{17,1},{2,18},{18,2},{3,19},{19,3},{4,20},{20... | collective-permute-start | bytes 1572872 | tf_op jit(solution)/shard_map/ppermute | solution.py:251
  (65 other events, 412.6 us)
Sparse Core Ops, SparseCore 0:
  10.2 53.0 all-gather.14
  86.9 51.2 all-gather.12
  170.3 73.5 reduce-scatter.6
  247.6 72.0 reduce-scatter.8
  325.8 137.4 reduce-scatter.10
  465.4 138.9 reduce-scatter.12
  606.6 34.8 all-gather.10
  643.8 40.9 all-gather.8

commit v2 on v1

--- a/solution.py
+++ b/solution.py
@@ -230,13 +230,30 @@
 
 def gather_dp(local_part):
     dp_count = lax.axis_size("dp")
-    if dp_count != 2:
+    owner_count = lax.axis_size("expert")
+    if dp_count != 2 or owner_count % 2:
         return lax.all_gather(local_part, "dp", axis=0, tiled=True)
-    other = lax.ppermute(local_part, "dp", [(0, 1), (1, 0)])
+    low, high = jnp.split(local_part, 2, 0)
+    even = lax.axis_index("expert") % 2 == 0
+    near = lax.ppermute(jnp.where(even, low, high), "dp", [(0, 1), (1, 0)])
+    far = lax.ppermute(near, "expert", [(i, i ^ 1) for i in range(owner_count)])
+    other = jnp.concatenate([jnp.where(even, near, far), jnp.where(even, far, near)], 0)
     first = lax.axis_index("dp") == 0
     return jnp.concatenate(
         [jnp.where(first, local_part, other), jnp.where(first, other, local_part)], 0
     )
+
+
+def all_sums(partial):
+    owner_count = lax.axis_size("expert")
+    dp_count = lax.axis_size("dp")
+    width = partial.shape[1]
+    pieces = partial.astype(jnp.bfloat16).reshape(dp_count, owner_count, -1, width)
+    piece = lax.psum_scatter(
+        pieces.transpose(1, 0, 2, 3).reshape(-1, width), "expert", scatter_dimension=0, tiled=True
+    )
+    piece = scatter_dp(piece, 0).astype(jnp.bfloat16)
+    return lax.all_gather(piece, "expert", axis=0, tiled=True).astype(jnp.float32)
 
 
 def scatter_dp(partial, axis):
@@ -250,11 +267,6 @@
     first = lax.axis_index("dp") == 0
     arrived = lax.ppermute(jnp.where(first, high, low), "dp", [(0, 1), (1, 0)])
     return jnp.where(first, low, high).astype(jnp.float32) + arrived.astype(jnp.float32)
-
-
-def two_parts(values):
-    high = lax.reduce_precision(values, 8, 7)
-    return (high.astype(jnp.bfloat16), (values - high).astype(jnp.bfloat16))
 
 
 def shards(
@@ -290,9 +302,12 @@
     router_mat = small_mat[:, :expert_count]
     gain_first = small_mat[:, expert_count]
     gain_second = small_mat[:, expert_count + 1]
-    query_mat = gather_dp(query_weight)
-    key_matrix = gather_dp(key_projection_weight)
-    value_matrix = gather_dp(value_projection_weight)
+    joined_mat = gather_dp(
+        jnp.concatenate([query_weight, key_projection_weight, value_projection_weight], 1)
+    )
+    query_mat = joined_mat[:, :query_width]
+    key_matrix = joined_mat[:, query_width : query_width + key_width]
+    value_matrix = joined_mat[:, query_width + key_width :]
     out_mat = gather_dp(out_weight)
 
     routes_all = lax.all_gather(routes, "expert")
@@ -312,9 +327,26 @@
         rows = product("lsct,std->lscd", pick, gathered)
         return rows.reshape(local_count, owner_count * capacity, model_width)
 
-    def tokens_of(rows):
-        shaped = rows.reshape(local_count, owner_count, capacity, rows.shape[-1])
-        return product("lsct,lscd->std", pick, shaped).astype(jnp.bfloat16)
+    own_hot = (routes[:, :, None] == jnp.arange(expert_count, dtype=jnp.int32)).any(1)
+    own_rank = matrix_multiply(before.T, own_hot.astype(jnp.bfloat16)).astype(jnp.int32)
+    own_slot = jnp.where(own_hot, own_rank, -1)
+    own_pick = (
+        own_slot[:, :, None] == jnp.arange(capacity, dtype=jnp.int32)[None, None, :]
+    ).astype(jnp.bfloat16)
+
+    def send_back(rows):
+        shaped = rows.reshape(local_count, owner_count, capacity, model_width)
+        return lax.all_to_all(
+            shaped.transpose(1, 0, 2, 3).reshape(expert_count, capacity, model_width),
+            "expert",
+            split_axis=0,
+            concat_axis=0,
+            tiled=True,
+        )
+
+    def sum_back(returned):
+        flat = returned.reshape(expert_count * capacity, model_width)
+        return matrix_multiply(own_pick.reshape(token_rows, expert_count * capacity), flat)
 
     hidden, saved = mixer_forward(
         tokens, segments, gain_first, query_mat, key_matrix, value_matrix, out_mat
@@ -341,45 +373,37 @@
         local_count, owner_count, capacity
     )
     token_grad_prob = jnp.sum(jnp.where(picked, row_grad_prob[..., None], 0.0), 2)
-    dense_grad_prob = jnp.sum(
-        token_grad_prob[..., None] * my_column[:, None, None, :], 0
-    )
-    high_part, low_part = two_parts(dense_grad_prob)
-    forward_send = jnp.concatenate([tokens_of(weighted), high_part, low_part], -1)
-    forward_sum = lax.psum_scatter(
-        forward_send.reshape(owner_count * token_rows, -1),
+    back_prob = lax.all_to_all(
+        token_grad_prob.transpose(1, 0, 2).reshape(expert_count, token_rows),
         "expert",
-        scatter_dimension=0,
+        split_axis=0,
+        concat_axis=0,
         tiled=True,
-    ).astype(jnp.float32)
-    output = (hidden + forward_sum[:, :model_width]).astype(jnp.bfloat16)
-    dense_back = (
-        forward_sum[:, model_width : model_width + expert_count]
-        + forward_sum[:, model_width + expert_count :]
-    )
-    grad_prob = jnp.sum(chosen_hot * dense_back[:, None, :], -1)
+    )
+    grad_prob = jnp.sum(chosen_hot * back_prob.T[:, None, :], -1)
     grad_output = cotangent.astype(jnp.float32)
 
     grad_rows = (row_prob * cotangent_rows).astype(jnp.bfloat16)
     grad_owner_rows, gate_grad, up_grad, down_grad = expert_backward(
         grad_rows, owner_rows, kept_acts, gate_weight, up_weight, down_weight
     )
-    backward_sum = lax.psum_scatter(
-        tokens_of(grad_owner_rows).reshape(owner_count * token_rows, -1),
-        "expert",
-        scatter_dimension=0,
-        tiled=True,
-    )
+    grad_back = send_back(grad_owner_rows)
     expert_shares = (
         scatter_dp(gate_grad, 1),
         scatter_dp(up_grad, 1),
         scatter_dp(down_grad, 2),
     )
+    grad_back, expert_shares, weighted = lax.optimization_barrier(
+        (grad_back, expert_shares, weighted)
+    )
+    forward_back = send_back(weighted)
+    output = (hidden + sum_back(forward_back)).astype(jnp.bfloat16)
+    backward_sum = sum_back(grad_back)
     router_grad = route_back(route_prob, grad_prob, chosen_hot)
-    grad_expert_input = backward_sum.astype(jnp.float32) + matrix_multiply(
+    grad_expert_input = backward_sum + matrix_multiply(
         router_grad, router_mat.T
     )
-    router_wgrad = matrix_multiply(expert_input.T, router_grad)
+    router_wgrad = matrix_multiply(router_grad.T, expert_input)
     grad_normed, second_gain_grad = normalize_back(
         grad_expert_input, normed_second, factor_second, gain_second
     )
@@ -388,41 +412,30 @@
         grad_hidden, saved, gain_first, query_mat, key_matrix, value_matrix, out_mat
     )
 
-    def total(partial):
-        piece = lax.psum_scatter(
-            partial.astype(jnp.bfloat16), ("dp", "expert"), scatter_dimension=0, tiled=True
-        )
-        return lax.all_gather(piece, "expert", axis=0, tiled=True)
-
-    out_share = total(out_wgrad).astype(jnp.float32)
-    joined = total(
-        jnp.concatenate(
-            [
-                query_wgrad,
-                key_wgrad,
-                value_wgrad,
-                router_wgrad,
-                first_gain_grad[:, None],
-                second_gain_grad[:, None],
-            ],
-            1,
-        )
+    out_share = all_sums(out_wgrad)
+    joined = all_sums(jnp.concatenate([query_wgrad, key_wgrad, value_wgrad], 1))
+    query_share = joined[:, :query_width]
+    key_share = joined[:, query_width : query_width + key_width]
+    value_share = joined[:, query_width + key_width :]
+    extras = jnp.concatenate(
+        [router_wgrad, first_gain_grad[None, :], second_gain_grad[None, :]], 0
+    )
+    extras = lax.psum(extras.astype(jnp.bfloat16), ("dp", "expert"))
+    extras = lax.dynamic_slice_in_dim(
+        extras, lax.axis_index("dp") * row_part, row_part, 1
     ).astype(jnp.float32)
-    cuts = []
-    start = 0
-    for width in (query_width, key_width, key_width, expert_count, 1, 1):
-        cuts.append(joined[:, start : start + width])
-        start += width
-    query_share, key_share, value_share, router_share, first_share, second_share = cuts
+    router_share = extras[:expert_count].T
+    first_share = extras[expert_count]
+    second_share = extras[expert_count + 1]
     return (
         output,
         grad_tokens,
-        first_share.reshape(row_part),
+        first_share,
         query_share,
         key_share,
         value_share,
         out_share,
-        second_share.reshape(row_part),
+        second_share,
         router_share,
         expert_shares[0],
         expert_shares[1],

time: 701 us -> 506 us (0.72)
  waiting for transfers between devices: 494 us -> 239 us
  blocking collectives: 40.7 us -> 81.2 us
  starting transfers between devices: 11.4 us -> 28.5 us
  local copies, waits for them, and re-layouts: 44.7 us -> 35.5 us
    reduce_scatter x4 -> x2, waiting for transfers between devices: 380 us -> 142 us  [all_sums(): lax.psum_scatter(pieces.transpose(1, 0, 2, 3).reshape(-1, width), 'expert...]
    psum x0 -> x1, blocking collectives: none -> 39.9 us  [shards(): extras = lax.psum(extras.astype(jnp.bfloat16), ('dp', 'expert'))]
    concatenate x2 -> x1, local copies, waits for them, and re-layouts: 22.6 us -> 0.05 us  [shards(): jnp.concatenate([query_weight, key_projection_weight, value_projection_we...]
    ppermute x5 -> x6, waiting for transfers between devices: 50.3 us -> 31.9 us  [the longest x3 30.9 us: gather_dp(): near = lax.ppermute(jnp.where(even, low, high), 'dp', [(0, 1), (1, 0)])]
    all_to_all x0 -> x3, starting transfers between devices: none -> 15.5 us  [the longest x2 10.9 us: send_back(): lax.all_to_all(shaped.transpose(1, 0, 2, 3).reshape(expert_count, capacit...]
    all_gather x2, waiting for transfers between devices: 40.5 us -> 26.3 us  [all_sums(): lax.all_gather(piece, 'expert', axis=0, tiled=True).astype(jnp.float32)]
    ppermute x3 -> x5, waiting for transfers between devices: 22.2 us -> 30.7 us  [scatter_dp(): arrived = lax.ppermute(jnp.where(first, high, low), 'dp', [(0, 1), (1, 0)])]
    dot_general x15 -> x18, matrix products: 17.2 us -> 20.4 us  [matrix_multiply(): return jnp.dot(left_op, right_op, preferred_element_type=jnp.float32)]
  transfers between devices with their start and end apart: 16 -> 20, of which waited for: 13 -> 12; matrix products, arithmetic and copies ran while one was open for 13% -> 20% of each run, Pallas kernels for 0% -> 0%
where the time goes in v2:
time: 506 us; the launch traced here: 499 us
  waiting for transfers between devices  239 us (47%)
  blocking collectives  81.2 us (16%)
  matrix products  61.5 us (12%)
  other arithmetic  38.5 us (8%)
  local copies, waits for them, and re-layouts  35.5 us (7%)
  starting transfers between devices  28.5 us (6%)
  between operations  15.5 us (3%)
    reduce_scatter x2, waiting for transfers between devices, all_sums(): lax.psum_scatter(pieces.transpose(1, 0, 2, 3).reshape(-1, width), 'expert...  142 us
    dot_general x18, matrix products, product(): jnp.einsum(pattern, left_op, right_op, preferred_element_type=jnp.float32)  41.1 us
    psum x1, blocking collectives, shards(): extras = lax.psum(extras.astype(jnp.bfloat16), ('dp', 'expert'))  39.9 us
    ppermute x3, waiting for transfers between devices, gather_dp(): near = lax.ppermute(jnp.where(even, low, high), 'dp', [(0, 1), (1, 0)])  30.9 us
    ppermute x5, waiting for transfers between devices, scatter_dp(): arrived = lax.ppermute(jnp.where(first, high, low), 'dp', [(0, 1), (1, 0)])  30.7 us
    all_gather x2, waiting for transfers between devices, all_sums(): lax.all_gather(piece, 'expert', axis=0, tiled=True).astype(jnp.float32)  26.3 us
    all_gather x1, blocking collectives, shards(): routes_all = lax.all_gather(routes, 'expert')  22.4 us
    dot_general x18, matrix products, matrix_multiply(): return jnp.dot(left_op, right_op, preferred_element_type=jnp.float32)  20.4 us
  transfers between devices with their start and end apart: 20, of which 12 were waited for; matrix products, arithmetic and copies ran while one was open for 20% of the time, Pallas kernels for 0%

profile of v2, /device:TPU:0, one launch (start us, length us, event | category | flops | bytes accessed | tf_op | source)
XLA Modules:
  0.0 499.4 jit_solution(8947114508440492954)
XLA Ops:
  11.0 3.1 collective-permute-start.2
  17.9 20.4 %collective-permute-done = bf16[256,18]{0,1:T(8,128)(2,1)S(1)} collective-permute-done((bf16[256,18]{0,1:T(8,128)(2,1)S(1)}, bf16[256,18]{0,1:T(8,128)(2,1)S(1)}, u32[]{:S(2)}, u32[]{:S(2)}) %collective-permute-start) | collective-permute-done | bytes 9248 | tf_op jit(solution)/shard_map/ppermute | solution.py:238
  38.3 10.5 %collective-permute-done.4 = bf16[256,1024]{1,0:T(8,128)(2,1)} collective-permute-done((bf16[256,1024]{1,0:T(8,128)(2,1)S(1)}, bf16[256,1024]{1,0:T(8,128)(2,1)}, u32[]{:S(2)}, u32[]{:S(2)}) %collective-permute-start.4) | collective-permute-done | bytes 524320 | tf_op jit(solution)/shard_map/ppermute | solution.py:238
  72.8 22.4 %all-gather = s32[2048,8]{0,1:T(8,128)S(1)} all-gather(s32[128,8]{0,1:T(8,128)} %param.16), channel_id=2, replica_groups=mesh['dp'=2,'expert'=16] {'expert'}, dimensions={0}, use_global_device_ids=true | all-gather | bytes 69632 | tf_op jit(solution)/shard_map/all_gather | solution.py:313
  102.3 18.9 %all-gather.1 = f32[2048,16]{0,1:T(8,128)S(1)} all-gather(f32[128,16]{0,1:T(8,128)S(1)} %select_reduce_fusion.4), channel_id=3, replica_groups=mesh['dp'=2,'expert'=16] {'expert'}, dimensions={0}, use_global_device_ids=true | all-gather | bytes 139264 | tf_op jit(solution)/shard_map/all_gather | solution.py:358
  122.6 5.5 %bitcast_convert_fusion = f32[1,16,80,1024]{3,2,1,0:T(8,128)} fusion(bf16[16,128,1024]{2,1,0:T(8,128)(2,1)} %bitcast.242, s32[16,128]{1,0:T(8,128)} %fusion.29), kind=kOutput, calls=%fused_computation.13 | convolution fusion | flops 338329600 | bytes 9445376 | tf_op jit(solution)/shard_map/lsct,std->lscd/dot_general | solution.py:19
  128.0 5.9 %copy.97 = f32[1280,1024]{0,1:T(8,128)} copy(f32[1280,1024]{1,0:T(8,128)} %bitcast.229) | data formatting | bytes 10485760 | tf_op jit(solution)/shard_map/convert_element_type | solution.py:368
  134.0 3.1 convolution_convert_fusion.1
  139.1 3.4 multiply_convert_fusion.3
  142.5 3.9 fusion.1
  149.7 4.6 all-to-all-start.2
  155.6 6.8 %multiply_convert_fusion.4 = (bf16[1280,512]{1,0:T(8,128)(2,1)S(1)}, bf16[1280,512]{1,0:T(8,128)(2,1)S(1)}) fusion(f32[1280,512]{1,0:T(8,128)} %copy-done.81, f32[1280,512]{1,0:T(8,128)} %get-tuple-element.66, bf16[1,512,1024]{2,1,0:T(8,128)(2,1)S(1)} %copy-done, f32[1,1280,1,1,1,1,1024]{6,1,5,4,3,2,0:T(8,128)} %bitcast.230, f32[1280]{0:T(1024)} %mul.545), kind=kOutput, calls=%fused_computation.16 | convolution fusion | flops 1353318400 | bytes 14160896 | tf_op jit(solution)/shard_map/erd,efd->erf/dot_general | solution.py:19
  164.5 3.1 add_convert_fusion
  167.5 6.2 %all-to-all-start = ((bf16[16,80,1024]{2,1,0:T(8,128)(2,1)}), bf16[16,80,1024]{2,1,0:T(8,128)(2,1)}, u32[]{:S(2)}, u32[]{:S(2)}) async-start(bf16[16,80,1024]{2,1,0:T(8,128)(2,1)} %bitcast.232), calls=%async_computation | async-start | bytes 5242880 | tf_op jit(solution)/shard_map/all_to_all | solution.py:339
  174.7 4.6 fusion.11
  189.7 4.6 collective-permute-done.8
  195.4 10.1 %collective-permute-done.7 = bf16[1,512,512]{2,1,0:T(8,128)(2,1)S(1)} collective-permute-done((bf16[1,512,512]{2,1,0:T(8,128)(2,1)S(1)}, bf16[1,512,512]{2,1,0:T(8,128)(2,1)S(1)}, u32[]{:S(2)}, u32[]{:S(2)}) %collective-permute-start.7) | collective-permute-done | bytes 524320 | tf_op jit(solution)/shard_map/ppermute | solution.py:268
  206.7 9.5 %collective-permute-done.6 = bf16[1,512,512]{2,1,0:T(8,128)(2,1)S(1)} collective-permute-done((bf16[1,512,512]{2,1,0:T(8,128)(2,1)S(1)}, bf16[1,512,512]{2,1,0:T(8,128)(2,1)S(1)}, u32[]{:S(2)}, u32[]{:S(2)}) %collective-permute-start.6) | collective-permute-done | bytes 524320 | tf_op jit(solution)/shard_map/ppermute | solution.py:268
  217.3 6.6 %all-to-all-done = bf16[16,80,1024]{2,1,0:T(8,128)(2,1)} async-done(((bf16[16,80,1024]{2,1,0:T(8,128)(2,1)}), bf16[16,80,1024]{2,1,0:T(8,128)(2,1)}, u32[]{:S(2)}, u32[]{:S(2)}) %all-to-all-start) | async-done | bytes 2621472 | tf_op jit(solution)/shard_map/all_to_all | solution.py:339
  223.9 2.4 convolution_bitcast_fusion.1
  244.6 2.3 copy.109
  246.9 56.4 %reduce-scatter.5.cloned.1.call-done = bf16[64,1024]{1,0:T(8,128)(2,1)} async-done(((bf16[1024,1024]{1,0:T(8,128)(2,1)}), bf16[64,1024]{1,0:T(8,128)(2,1)}) %reduce-scatter.5.cloned.1.call-update) | async-done | bytes 131088 | tf_op jit(solution)/shard_map/reduce_scatter | solution.py:252
  305.7 2.8 collective-permute-done.10
  310.1 4.5 copy.98
  314.6 4.6 all-to-all-start.1
  319.4 85.9 %reduce-scatter.3.cloned.1.call-done = bf16[64,2048]{1,0:T(8,128)(2,1)} async-done(((bf16[1024,2048]{1,0:T(8,128)(2,1)}), bf16[64,2048]{1,0:T(8,128)(2,1)}) %reduce-scatter.3.cloned.1.call-update) | async-done | bytes 262160 | tf_op jit(solution)/shard_map/reduce_scatter | solution.py:252
  407.8 3.8 collective-permute-done.9
  413.5 39.9 %psum.7 = bf16[18,1024]{1,0:T(8,128)(2,1)S(1)} all-reduce(bf16[18,1024]{1,0:T(8,128)(2,1)S(1)} %pad_maximum_fusion.17), channel_id=1, replica_groups=mesh['dp'=2,'expert'=16] {'dp','expert'}, use_global_device_ids=true, to_apply=%region_21.22 | all-reduce | flops 18432 | bytes 73728 | tf_op jit(solution)/shard_map/psum | solution.py:423
  455.7 3.0 fusion.26
  458.8 2.8 convert_element_type.428
  461.6 26.3 %all-gather.9.cloned.1.call-done = bf16[512,2048]{1,0:T(8,128)(2,1)} async-done(((bf16[32,2048]{1,0:T(8,128)(2,1)}), bf16[512,2048]{1,0:T(8,128)(2,1)}) %all-gather.9.cloned.1.call-update) | async-done | bytes 2097168 | tf_op jit(solution)/shard_map/all_gather | solution.py:256
  487.8 3.0 fusion.91
  (304 shorter events, 93.2 us)
Async XLA Ops:
  7.2 135.3 %copy-start = (bf16[1,512,1024]{2,1,0:T(8,128)(2,1)S(1)}, bf16[1,512,1024]{2,1,0:T(8,128)(2,1)}, u32[]{:S(2)}) copy-start(bf16[1,512,1024]{2,1,0:T(8,128)(2,1)} %param.26) | copy-start | bytes 3145732
  7.2 115.3 %all-gather.13.cloned.1.call-start = ((), (), s32[]{:S(2)}) async-start(), calls=%async_computation.9 | async-start | bytes 4456448 | tf_op jit(solution)/shard_map/all_gather | solution.py:314
  7.9 126.0 %all-gather.15.cloned.1.call-start = ((), (), s32[]{:S(2)}) async-start(), calls=%async_computation.10 | async-start | bytes 4456448 | tf_op jit(solution)/shard_map/all_gather | solution.py:355
  10.8 6.9 %copy-start.9 = (bf16[128,1024]{1,0:T(8,128)(2,1)S(1)}, bf16[128,1024]{1,0:T(8,128)(2,1)}, u32[]{:S(2)}) copy-start(bf16[128,1024]{1,0:T(8,128)(2,1)} %param.14) | copy-start | bytes 786436
  11.0 37.8 %collective-permute-start.2 = (bf16[256,2048]{1,0:T(8,128)(2,1)S(1)}, bf16[256,2048]{1,0:T(8,128)(2,1)}, u32[]{:S(2)}, u32[]{:S(2)}) collective-permute-start(bf16[256,2048]{1,0:T(8,128)(2,1)S(1)} %slice_select_fusion), channel_id=1, source_target_pairs={{0,16},{16,0},{1,17},{17,1},{2,18},{18,2},{3,19},{19,3},{4,20},{20... | collective-permute-start | bytes 3145736 | tf_op jit(solution)/shard_map/ppermute | solution.py:238
  14.1 24.2 %collective-permute-start = (bf16[256,18]{0,1:T(8,128)(2,1)S(1)}, bf16[256,18]{0,1:T(8,128)(2,1)S(1)}, u32[]{:S(2)}, u32[]{:S(2)}) collective-permute-start(bf16[256,18]{0,1:T(8,128)(2,1)S(1)} %slice_select_fusion.2), channel_id=1, source_target_pairs={{0,16},{16,0},{1,17},{17,1},{2,18},{18,2},{3,19},{19,3},{4,20},{20... | collective-permute-start | bytes 27656 | tf_op jit(solution)/shard_map/ppermute | solution.py:238
  14.3 34.5 %collective-permute-start.4 = (bf16[256,1024]{1,0:T(8,128)(2,1)S(1)}, bf16[256,1024]{1,0:T(8,128)(2,1)}, u32[]{:S(2)}, u32[]{:S(2)}) collective-permute-start(bf16[256,1024]{1,0:T(8,128)(2,1)S(1)} %slice_select_fusion.1), channel_id=1, source_target_pairs={{0,16},{16,0},{1,17},{17,1},{2,18},{18,2},{3,19},{19,3},{4,20},{20... | collective-permute-start | bytes 1572872 | tf_op jit(solution)/shard_map/ppermute | solution.py:238
  38.3 11.0 %collective-permute-start.1 = (bf16[256,18]{0,1:T(8,128)(2,1)S(1)}, bf16[256,18]{0,1:T(8,128)(2,1)S(1)}, u32[]{:S(2)}, u32[]{:S(2)}) collective-permute-start(bf16[256,18]{0,1:T(8,128)(2,1)S(1)} %collective-permute-done), channel_id=1, source_target_pairs={{0,1},{1,0},{2,3},{3,2},{4,5},{5,4},{6,7},{7,6},{8,9},{9,8},{10,11... | collective-permute-start | bytes 27656 | tf_op jit(solution)/shard_map/ppermute | solution.py:239
  48.8 2.3 collective-permute-start.5
  48.8 5.5 %collective-permute-start.3 = (bf16[256,2048]{1,0:T(8,128)(2,1)}, bf16[256,2048]{1,0:T(8,128)(2,1)}, u32[]{:S(2)}, u32[]{:S(2)}) collective-permute-start(bf16[256,2048]{1,0:T(8,128)(2,1)} %collective-permute-done.2), channel_id=1, source_target_pairs={{0,1},{1,0},{2,3},{3,2},{4,5},{5,4},{6,7},{7,6},{8,9},{9,8},{10,11... | collective-permute-start | bytes 3145736 | tf_op jit(solution)/shard_map/ppermute | solution.py:239
  49.3 10.1 %copy-start.66 = (f32[128]{0:T(128)}, f32[128]{0:T(128)S(1)}, u32[]{:S(2)}) copy-start(f32[128]{0:T(128)S(1)} %add_rsqrt_fusion.1) | copy-start | bytes 1540
  50.0 9.4 %copy-start.55 = (f32[1024,1]{0,1:T(1,128)}, f32[1024,1]{0,1:T(1,128)S(1)}, u32[]{:S(2)}) copy-start(f32[1024,1]{0,1:T(1,128)S(1)} %get-tuple-element.54) | copy-start | bytes 12292
  149.7 17.9 %all-to-all-start.2 = ((f32[16,1,128]{2,1,0:T(1,128)}), f32[16,1,128]{2,1,0:T(1,128)}, u32[]{:S(2)}, u32[]{:S(2)}) async-start(f32[16,1,128]{2,1,0:T(1,128)} %bitcast.277), calls=%async_computation.2 | async-start | bytes 16384 | tf_op jit(solution)/shard_map/all_to_all | solution.py:376
  155.6 6.8 %copy-start.78 = (bf16[1,1024,512]{2,1,0:T(8,128)(2,1)S(1)}, bf16[1,1024,512]{2,1,0:T(8,128)(2,1)}, u32[]{:S(2)}) copy-start(bf16[1,1024,512]{2,1,0:T(8,128)(2,1)} %param.24) | copy-start | bytes 3145732
  167.5 56.4 %all-to-all-start = ((bf16[16,80,1024]{2,1,0:T(8,128)(2,1)}), bf16[16,80,1024]{2,1,0:T(8,128)(2,1)}, u32[]{:S(2)}, u32[]{:S(2)}) async-start(bf16[16,80,1024]{2,1,0:T(8,128)(2,1)} %bitcast.232), calls=%async_computation | async-start | bytes 5242880 | tf_op jit(solution)/shard_map/all_to_all | solution.py:339
  173.8 129.6 %reduce-scatter.5.cloned.1.call-start = ((), (), s32[]{:S(2)}) async-start(), calls=%async_computation.7 | async-start | bytes 2228224 | tf_op jit(solution)/shard_map/reduce_scatter | solution.py:252
  179.4 14.9 %collective-permute-start.8 = (bf16[1,512,512]{2,1,0:T(8,128)(2,1)S(1)}, bf16[1,512,512]{2,1,0:T(8,128)(2,1)S(1)}, u32[]{:S(2)}, u32[]{:S(2)}) collective-permute-start(bf16[1,512,512]{2,1,0:T(8,128)(2,1)S(1)} %broadcast_select_fusion.6), channel_id=1, source_target_pairs={{0,16},{16,0},{1,17},{17,1},{2,18},{18,2},{3,19},{19,3},{4,20},{20... | collective-permute-start | bytes 1572872 | tf_op jit(solution)/shard_map/ppermute | solution.py:268
  182.5 23.0 %collective-permute-start.7 = (bf16[1,512,512]{2,1,0:T(8,128)(2,1)S(1)}, bf16[1,512,512]{2,1,0:T(8,128)(2,1)S(1)}, u32[]{:S(2)}, u32[]{:S(2)}) collective-permute-start(bf16[1,512,512]{2,1,0:T(8,128)(2,1)S(1)} %broadcast_select_fusion.7), channel_id=1, source_target_pairs={{0,16},{16,0},{1,17},{17,1},{2,18},{18,2},{3,19},{19,3},{4,20},{20... | collective-permute-start | bytes 1572872 | tf_op jit(solution)/shard_map/ppermute | solution.py:268
  184.8 31.3 %collective-permute-start.6 = (bf16[1,512,512]{2,1,0:T(8,128)(2,1)S(1)}, bf16[1,512,512]{2,1,0:T(8,128)(2,1)S(1)}, u32[]{:S(2)}, u32[]{:S(2)}) collective-permute-start(bf16[1,512,512]{2,1,0:T(8,128)(2,1)S(1)} %broadcast_select_fusion.8), channel_id=1, source_target_pairs={{0,16},{16,0},{1,17},{17,1},{2,18},{18,2},{3,19},{19,3},{4,20},{20... | collective-permute-start | bytes 1572872 | tf_op jit(solution)/shard_map/ppermute | solution.py:268
  206.7 19.6 %copy-start.15 = (f32[128,1024]{1,0:T(8,128)S(1)}, f32[128,1024]{1,0:T(8,128)}, u32[]{:S(2)}) copy-start(f32[128,1024]{1,0:T(8,128)} %copy-done.14) | copy-start | bytes 1572868
  232.9 172.4 %reduce-scatter.3.cloned.1.call-start = ((), (), s32[]{:S(2)}) async-start(), calls=%async_computation.5 | async-start | bytes 4456448 | tf_op jit(solution)/shard_map/reduce_scatter | solution.py:252
  246.9 211.9 %all-gather.11.cloned.1.call-start = ((), (), s32[]{:S(2)}) async-start(), calls=%async_computation.8 | async-start | bytes 1114112 | tf_op jit(solution)/shard_map/all_gather | solution.py:256
  304.2 4.3 collective-permute-start.10
  314.6 98.7 %copy-start.21 = (bf16[128,1024]{1,0:T(8,128)(2,1)S(1)}, bf16[128,1024]{1,0:T(8,128)(2,1)}, u32[]{:S(2)}) copy-start(bf16[128,1024]{1,0:T(8,128)(2,1)} %multiply_convert_fusion.10) | copy-start | bytes 786436
  314.6 98.7 %copy-start.62 = (bf16[128,16]{0,1:T(8,128)(2,1)S(1)}, bf16[128,16]{0,1:T(8,128)(2,1)}, u32[]{:S(2)}) copy-start(bf16[128,16]{0,1:T(8,128)(2,1)} %select_reduce_fusion.2) | copy-start | bytes 12292
  314.6 98.8 %copy-start.69 = (bf16[1024]{0:T(1024)(128)(2,1)S(1)}, bf16[1024]{0:T(1024)(128)(2,1)}, u32[]{:S(2)}) copy-start(bf16[1024]{0:T(1024)(128)(2,1)} %get-tuple-element.22) | copy-start | bytes 6148
  314.6 140.1 %copy-start.18 = (f32[128,1024]{1,0:T(8,128)S(1)}, f32[128,1024]{1,0:T(8,128)}, u32[]{:S(2)}) copy-start(f32[128,1024]{1,0:T(8,128)} %copy-done.17) | copy-start | bytes 1572868
  314.6 141.1 %all-to-all-start.1 = ((bf16[16,80,1024]{2,1,0:T(8,128)(2,1)}), bf16[16,80,1024]{2,1,0:T(8,128)(2,1)}, u32[]{:S(2)}, u32[]{:S(2)}) async-start(bf16[16,80,1024]{2,1,0:T(8,128)(2,1)} %bitcast.233), calls=%async_computation.1 | async-start | bytes 5242880 | tf_op jit(solution)/shard_map/all_to_all | solution.py:339
  319.3 136.5 %copy-start.16 = (f32[128,1024]{1,0:T(8,128)S(1)}, f32[128,1024]{1,0:T(8,128)}, u32[]{:S(2)}) copy-start(f32[128,1024]{1,0:T(8,128)} %copy-done.14) | copy-start | bytes 1572868
  319.3 136.4 %copy-start.63 = (s32[128,16]{0,1:T(8,128)S(1)}, s32[128,16]{0,1:T(8,128)}, u32[]{:S(2)}) copy-start(s32[128,16]{0,1:T(8,128)} %fusion.30) | copy-start | bytes 24580
  319.3 168.5 %all-gather.9.cloned.1.call-start = ((), (), s32[]{:S(2)}) async-start(), calls=%async_computation.6 | async-start | bytes 2228224 | tf_op jit(solution)/shard_map/all_gather | solution.py:256
  406.2 5.4 %collective-permute-start.9 = (bf16[32,2048]{1,0:T(8,128)(2,1)S(1)}, bf16[32,2048]{1,0:T(8,128)(2,1)S(1)}, u32[]{:S(2)}, u32[]{:S(2)}) collective-permute-start(bf16[32,2048]{1,0:T(8,128)(2,1)S(1)} %broadcast_select_fusion.11), channel_id=1, source_target_pairs={{0,16},{16,0},{1,17},{17,1},{2,18},{18,2},{3,19},{19,3},{4,20},{20... | collective-permute-start | bytes 393224 | tf_op jit(solution)/shard_map/ppermute | solution.py:268
  (72 other events, 202.7 us)
Sparse Core Ops, SparseCore 0:
  10.2 53.0 all-gather.12
  72.9 53.0 all-gather.14
  233.0 70.3 reduce-scatter.4
  307.0 98.1 reduce-scatter.2
  407.8 36.9 all-gather.10
  447.4 40.4 all-gather.8
